TPU v7x, 32 devices: a whole 2x2x4 slice. The times are simulated.
32 devices in a mesh: lat: 4 (over y, core), lon: 8 (over z, x).
Axes of the slice: x: 2, y: 2, z: 4, core: 2. Of those that a mesh axis runs over, the one named last changes fastest.
Arguments:
- state: float32 [4, 8, 448, 4096], P(None, None, 'lat', 'lon'), may hold values from -6 to 6
- level_courant: float32 [8], replicated, may hold values from 0.05 to 0.3
- damp_table: float32 [16, 2048], replicated, may hold values from 0.05 to 1
- row_flag: int32 [448], P('lat'), may hold values from 0 to 1, as said below
- row_table: int32 [448], P('lat'), may hold values from 0 to 15
- partner: int32 [4096], P('lon'), may hold values from 0 to 4095, each once
Outputs:
- new_state: float32 [4, 8, 448, 4096], P(None, None, 'lat', 'lon')
Inputs may be any that keep to these rules, and one draw needn't show every extreme that they name: `row_flag`: 0 on every row from 112 to 335; each row of the outer quarters is 1 or 0 on its own; the first and the last row are 1. `partner`: a permutation of the columns.
All inputs are finite; a program needn't handle non-finite values.
Results may differ from a plain program's by a relative error of at most 0.00005.
Values sent between devices are 32-bit elements; how exact they have to be, the bound alone decides.
A program may use at most 128 MiB of HBM per device.

v0:
```python
import math

import jax
import jax.numpy as jnp
from jax import lax
from jax.sharding import PartitionSpec as P

coriolis = 0.3
cos_floor = 0.25


def extended(cells, sides, width, closed):
    for axis, dim in sides:
        count = lax.axis_size(axis)
        ends = count if closed else count - 1
        head = lax.slice_in_dim(cells, 0, width, axis=dim)
        tail = lax.slice_in_dim(cells, cells.shape[dim] - width, cells.shape[dim], axis=dim)
        cells = jnp.concatenate(
            [
                lax.ppermute(tail, axis, [(i, (i + 1) % count) for i in range(ends)]),
                cells,
                lax.ppermute(head, axis, [((i + 1) % count, i) for i in range(ends)]),
            ],
            axis=dim,
        )
    return cells


def zonal_pair(stack):
    padded = extended(stack, (("lon", 3),), 1, True)
    return (padded[..., 2:], padded[..., :-2])


def meridional(stack, sign, partner):
    padded = extended(stack, (("lat", 2),), 1, False)
    edge_rows = jnp.concatenate([stack[:, :, :1, :], stack[:, :, -1:, :]], axis=2)
    circle = lax.all_gather(edge_rows, "lon", axis=3, tiled=True)
    across = sign * jnp.take(circle, partner, axis=3)
    southward = padded[:, :, :-2, :]
    northward = padded[:, :, 2:, :]
    at_south = lax.axis_index("lat") == 0
    at_north = lax.axis_index("lat") == lax.axis_size("lat") - 1
    southward = southward.at[:, :, 0, :].set(
        jnp.where(at_south, across[:, :, 0, :], southward[:, :, 0, :])
    )
    northward = northward.at[:, :, -1, :].set(
        jnp.where(at_north, across[:, :, 1, :], northward[:, :, -1, :])
    )
    return (northward, southward)


def angle_table(size_a, size_b, modulus):
    product = (
        jnp.arange(size_a, dtype=jnp.int32)[:, None]
        * jnp.arange(size_b, dtype=jnp.int32)[None, :]
        % modulus
    )
    angle = product.astype(jnp.float32) * (2.0 * math.pi / modulus)
    return (jnp.cos(angle), jnp.sin(angle))


def fourier_damp(rows_in, damping):
    count_b, count_r, length = rows_in.shape
    inner_len = 128
    outer_len = length // inner_len
    highest = lax.Precision.HIGHEST
    small_cos, small_sin = angle_table(outer_len, outer_len, outer_len)
    twid_cos, twid_sin = angle_table(outer_len, inner_len, length)
    large_cos, large_sin = angle_table(inner_len, inner_len, inner_len)
    grid = rows_in.reshape(count_b, count_r, outer_len, inner_len)
    a_real = jnp.einsum("brpq,kp->brkq", grid, small_cos, precision=highest)
    a_imag = -jnp.einsum("brpq,kp->brkq", grid, small_sin, precision=highest)
    b_real = a_real * twid_cos + a_imag * twid_sin
    b_imag = a_imag * twid_cos - a_real * twid_sin
    f_real = jnp.einsum("brkq,qm->brkm", b_real, large_cos, precision=highest) + jnp.einsum(
        "brkq,qm->brkm", b_imag, large_sin, precision=highest
    )
    f_imag = jnp.einsum("brkq,qm->brkm", b_imag, large_cos, precision=highest) - jnp.einsum(
        "brkq,qm->brkm", b_real, large_sin, precision=highest
    )
    weight = jnp.transpose(damping.reshape(count_r, inner_len, outer_len), (0, 2, 1))[None]
    f_real = f_real * weight
    f_imag = f_imag * weight
    z_real = jnp.einsum("brkq,qm->brkm", f_real, large_cos, precision=highest) - jnp.einsum(
        "brkq,qm->brkm", f_imag, large_sin, precision=highest
    )
    z_imag = jnp.einsum("brkq,qm->brkm", f_imag, large_cos, precision=highest) + jnp.einsum(
        "brkq,qm->brkm", f_real, large_sin, precision=highest
    )
    w_real = z_real * twid_cos - z_imag * twid_sin
    w_imag = z_imag * twid_cos + z_real * twid_sin
    result = jnp.einsum("brkq,kp->brpq", w_real, small_cos, precision=highest) - jnp.einsum(
        "brkq,kp->brpq", w_imag, small_sin, precision=highest
    )
    return (result / length).reshape(count_b, count_r, length)


def damp_half(values, row_codes, damp_table):
    active = jnp.any(row_codes > 0)

    def run_filter(inputs):
        table_count = damp_table.shape[0]
        row_count = row_codes.shape[0]
        pick = (row_codes[:, None] - 1 == jnp.arange(table_count, dtype=jnp.int32)[None, :]).astype(
            jnp.float32
        )
        half_damp = jnp.dot(
            pick, damp_table, precision=lax.Precision.HIGHEST, preferred_element_type=jnp.float32
        )
        full_damp = jnp.concatenate(
            [jnp.ones((row_count, 1), jnp.float32), half_damp, jnp.flip(half_damp[:, :-1], axis=1)],
            axis=1,
        )
        shaped = fourier_damp(inputs, full_damp)
        return jnp.where((row_codes > 0)[None, :, None], shaped, inputs)

    return lax.cond(active, run_filter, lambda kept: kept, values)


def regroup(row_block, row_codes, damp_table):
    fields_n, levels_n, rows_n, cols_n = row_block.shape
    half_rows = rows_n // 2
    merged = row_block.reshape(fields_n * levels_n, rows_n, cols_n)
    circles = lax.all_to_all(merged, "lon", split_axis=0, concat_axis=2, tiled=True)
    first_part = damp_half(circles[:, :half_rows, :], row_codes[:half_rows], damp_table)
    second_part = damp_half(circles[:, half_rows:, :], row_codes[half_rows:], damp_table)
    joined = jnp.concatenate([first_part, second_part], axis=1)
    returned = lax.all_to_all(joined, "lon", split_axis=2, concat_axis=0, tiled=True)
    return returned.reshape(fields_n, levels_n, rows_n, cols_n)


def per_device(state, level_courant, damp_table, row_flag, row_table, partner):
    fields_n, levels_n, rows_n, cols_n = state.shape
    whole_rows = rows_n * lax.axis_size("lat")
    row_pos = (lax.axis_index("lat") * rows_n + jnp.arange(rows_n, dtype=jnp.int32)).astype(
        jnp.float32
    )
    latitude = -jnp.pi / 2 + jnp.pi * (row_pos + 0.5) / whole_rows
    cos_lat = jnp.cos(latitude)[:, None]
    sin_lat = jnp.sin(latitude)[:, None]
    metric = 1.0 / jnp.maximum(cos_lat, cos_floor)
    courant = level_courant[:, None, None]
    pressure, wind_u, wind_v, thermo = (state[0], state[1], state[2], state[3])
    scalars = jnp.stack([pressure, thermo])
    eastward, westward = zonal_pair(scalars)
    northward, southward = meridional(scalars, 1.0, partner)
    tend_u = -courant * metric * (eastward[0] - westward[0]) * 0.5 + coriolis * sin_lat * wind_v
    tend_v = -courant * (northward[0] - southward[0]) * 0.5 - coriolis * sin_lat * wind_u
    u_new = wind_u + tend_u
    v_new = wind_v + tend_v
    flux = v_new * cos_lat
    u_east, u_west = zonal_pair(u_new[None])
    f_north, f_south = meridional(flux[None], -1.0, partner)
    divergence = (
        courant * metric * ((u_east[0] - u_west[0]) * 0.5 + (f_north[0] - f_south[0]) * 0.5)
    )
    tend_t = (
        -courant * metric * u_new * (eastward[1] - westward[1]) * 0.5
        - courant * v_new * (northward[1] - southward[1]) * 0.5
    )
    increments = jnp.stack([-divergence, tend_u, tend_v, tend_t])
    row_codes = jnp.where(row_flag == 1, row_table + 1, 0)
    increments = regroup(increments, row_codes, damp_table)
    return state + increments


def solution(mesh):
    placed = (P(None, None, "lat", "lon"), P(), P(), P("lat"), P("lat"), P("lon"))
    return jax.shard_map(
        per_device,
        mesh=mesh,
        in_specs=placed,
        out_specs=P(None, None, "lat", "lon"),
        check_vma=False,
    )
```

profile of v0, /device:TPU:10, one launch (start us, length us, event | category | flops | bytes accessed | tf_op | source)
XLA Modules:
  0.0 606.5 jit_solution(8997078380388542498)
XLA Ops:
  13.0 31.2 %all_gather.6 = f32[2,8,2,4096]{3,1,2,0:T(8,128)S(1)} all-gather(f32[2,8,2,512]{3,1,2,0:T(8,128)S(1)} %pad_maximum_fusion.14), channel_id=1, replica_groups=mesh['lat'=4,'lon'=8] {'lon'}, dimensions={3}, use_global_device_ids=true | all-gather | bytes 589824 | tf_op jit(solution)/shard_map/all_gather | solution.py:37
  44.2 7.9 %copy.330 = f32[2,8,2,4096]{1,2,3,0:T(2,128)} copy(f32[2,8,2,4096]{3,1,2,0:T(8,128)S(1)} %all_gather.6) | data formatting | bytes 1048576 | tf_op jit(solution)/shard_map/all_gather | solution.py:37
  52.1 5.5 gather_fusion
  60.3 6.4 %pad_maximum_fusion.4 = (f32[2,8,112,512]{3,2,1,0:T(8,128)}, f32[2,8,112,512]{3,2,1,0:T(8,128)}) fusion(f32[2,8,1,512]{3,2,1,0:T(1,128)S(1)} %collective-permute-done.4, f32[1,8,112,512]{3,2,1,0:T(8,128)} %copy-done.8, f32[1,8,112,512]{3,2,1,0:T(8,128)S(1)} %get-tuple-element.94, f32[2,8,1,512]{3,2,1,0:T(1,128)S(1)} %collective-permute-done.5), kind=kLoop, calls=%fused_computation.277 | loop fusion | flops 3670016 | bytes 11075584 | tf_op jit(solution)/shard_map/concatenate | solution.py:18
  70.3 5.4 broadcast_multiply_fusion
  81.3 30.3 %all_gather.7 = f32[1,8,2,4096]{3,1,2,0:T(8,128)S(1)} all-gather(f32[1,8,2,512]{3,1,2,0:T(8,128)S(1)} %pad_maximum_fusion.16), channel_id=1, replica_groups=mesh['lat'=4,'lon'=8] {'lon'}, dimensions={3}, use_global_device_ids=true | all-gather | bytes 294912 | tf_op jit(solution)/shard_map/all_gather | solution.py:37
  111.7 4.3 copy.334
  115.9 3.7 gather_fusion.1
  119.8 8.2 %fusion.262 = (f32[1,8,112,512]{3,2,1,0:T(8,128)}, f32[1,8,112,512]{3,2,1,0:T(8,128)S(1)}, f32[1,8,112,512]{3,2,1,0:T(8,128)}) fusion(f32[2,8,112,512]{3,2,1,0:T(8,128)} %scatter.15, f32[2,8,112,512]{3,2,1,0:T(8,128)} %scatter.14, f32[2,8,112,1]{3,2,1,0:T(8,128)} %copy.327, f32[1,8,112,512]{3,2,1,0:T(8,128)} %copy-done.8, ...), kind=kLoop, calls=%fused_computation.282 | loop fusion | flops 11010048 | bytes 18368480 | tf_op jit(solution)/shard_map/sub | solution.py:158
  135.0 8.4 %collective-permute-done.2 = f32[1,8,112,1]{3,2,1,0:T(8,128)S(1)} collective-permute-done((f32[1,8,112,1]{3,2,1,0:T(8,128)S(1)}, f32[1,8,112,1]{3,2,1,0:T(8,128)S(1)}, u32[]{:S(2)}, u32[]{:S(2)}) %collective-permute-start.2) | collective-permute-done | bytes 3616 | tf_op jit(solution)/shard_map/ppermute | solution.py:22
  146.4 4.2 fusion.276
  150.8 3.5 pad_maximum_fusion.1
  154.3 8.0 %all-to-all-start = ((f32[32,112,512]{2,1,0:T(8,128)}), f32[32,112,512]{2,1,0:T(8,128)}, u32[]{:S(2)}, u32[]{:S(2)}) async-start(f32[32,112,512]{2,1,0:T(8,128)} %bitcast.204), calls=%async_computation | async-start | bytes 14680064 | tf_op jit(solution)/shard_map/all_to_all | solution.py:124
  164.4 153.6 %all-to-all-done = f32[32,112,512]{2,1,0:T(8,128)} async-done(((f32[32,112,512]{2,1,0:T(8,128)}), f32[32,112,512]{2,1,0:T(8,128)}, u32[]{:S(2)}, u32[]{:S(2)}) %all-to-all-start) | async-done | bytes 7340064 | tf_op jit(solution)/shard_map/all_to_all | solution.py:124
  318.0 4.3 copy.364
  322.3 3.9 fusion.289
  326.2 76.2 %conditional.2 = (f32[4,56,4096]{1,0,2:T(4,128)}) conditional(s32[]{:T(128)} %convert_element_type.123, f32[4,56,4096]{2,1,0:T(8,128)} %get-tuple-element.92, (s32[56]{0:T(128)S(1)}, f32[4,56,4096]{2,1,0:T(8,128)}, f32[16,2048]{1,0:T(8,128)S(1)}) %tuple.62), branch_computations={%region_1.2_spmd, %region_2.3_spmd} | conditional | flops 12735988736 | bytes 230196096 | solution.py:117
  329.4 3.5 fusion
  333.0 3.5 fusion.2
  336.5 5.3 fusion.4
  346.5 7.7 %subtract_multiply_fusion = f32[4,56,32,128]{3,2,1,0:T(8,128)S(1)} fusion(f32[4,56,32,128]{3,2,1,0:T(8,128)} %fusion.4, f32[56,32,128]{2,1,0:T(8,128)S(1)} %copy.319, f32[32,4,56,128]{3,0,2,1:T(8,128)} %copy-done.2, f32[32,4,56,128]{3,0,2,1:T(8,128)} %copy-done, f32[32,128]{1,0:T(8,128)S(1)} %get-tuple-element.88, f32[32,128]{1,0:T(8,128)S(1)} %get-tuple-element.89), kind=kOutput, calls=%fused_computation.23 | convolution fusion | flops 1415020544 | bytes 15630336 | tf_op jit(solution)/shard_map/cond/branch_1_fun/brkq,qm->brkm/dot_general | solution.py:78
  357.5 3.4 fusion.6
  360.9 3.4 add_multiply_fusion
  364.4 3.7 convolution_add_fusion
  368.1 3.4 fusion.40
  378.2 5.2 multiply_bitcast_fusion
  383.5 4.8 reshape.392
  388.3 5.6 broadcast_select_fusion
  393.9 8.3 %copy.357 = f32[4,56,4096]{1,0,2:T(4,128)} copy(f32[4,56,4096]{2,1,0:T(8,128)} %broadcast_select_fusion) | data formatting | bytes 7340032 | tf_op jit(solution)/shard_map/cond | solution.py:117
  402.4 75.9 %conditional.3 = (f32[4,56,4096]{1,0,2:T(4,128)}) conditional(s32[]{:T(128)} %convert_element_type.125, f32[4,56,4096]{2,1,0:T(8,128)} %get-tuple-element.93, (s32[56]{0:T(128)S(1)}, f32[4,56,4096]{2,1,0:T(8,128)}, f32[16,2048]{1,0:T(8,128)S(1)}) %tuple.63), branch_computations={%region_4.5_spmd, %region_5.6_spmd} | conditional | flops 12735988736 | bytes 230196096 | solution.py:117
  405.2 3.5 fusion.130
  408.7 3.5 fusion.132
  412.2 5.2 fusion.134
  422.4 7.7 %subtract_multiply_fusion.1 = f32[4,56,32,128]{3,2,1,0:T(8,128)S(1)} fusion(f32[4,56,32,128]{3,2,1,0:T(8,128)} %fusion.134, f32[56,32,128]{2,1,0:T(8,128)S(1)} %copy.323, f32[32,4,56,128]{3,0,2,1:T(8,128)} %copy-done.6, f32[32,4,56,128]{3,0,2,1:T(8,128)} %copy-done.4, f32[32,128]{1,0:T(8,128)S(1)} %get-tuple-element.90, f32[32,128]{1,0:T(8,128)S(1)} %get-tuple-element.91), kind=kOutput, calls=%fused_computation.155 | convolution fusion | flops 1415020544 | bytes 15630336 | tf_op jit(solution)/shard_map/cond/branch_1_fun/brkq,qm->brkm/dot_general | solution.py:78
  433.4 3.4 fusion.136
  436.8 3.4 add_multiply_fusion.1
  440.2 3.4 convolution_add_fusion.1
  443.7 3.4 fusion.170
  447.1 3.4 convolution_subtract_fusion.1
  450.5 3.6 fusion.142
  454.1 5.3 multiply_bitcast_fusion.1
  459.4 4.8 reshape.395
  464.2 5.6 broadcast_select_fusion.1
  469.8 8.2 %copy.359 = f32[4,56,4096]{1,0,2:T(4,128)} copy(f32[4,56,4096]{2,1,0:T(8,128)} %broadcast_select_fusion.1) | data formatting | bytes 7340032 | tf_op jit(solution)/shard_map/cond | solution.py:117
  478.3 8.2 %pad_maximum_fusion = f32[4,112,4096]{1,0,2:T(4,128)S(1)} fusion(f32[4,56,4096]{1,0,2:T(4,128)} %get-tuple-element.80, f32[4,56,4096]{1,0,2:T(4,128)} %get-tuple-element.79), kind=kLoop, calls=%fused_computation.266 | loop fusion | flops 1835008 | bytes 14680064 | tf_op jit(solution)/shard_map/concatenate | solution.py:127
  486.5 99.6 %all_to_all.33 = f32[4,112,4096]{1,0,2:T(4,128)} all-to-all(f32[4,112,4096]{1,0,2:T(4,128)S(1)} %pad_maximum_fusion), channel_id=1, replica_groups=mesh['lat'=4,'lon'=8] {'lon'}, dimensions={2} | all-to-all | bytes 14680064 | tf_op jit(solution)/shard_map/all_to_all | solution.py:128
  586.1 9.5 %copy.339 = f32[8,4,112,512]{3,2,1,0:T(8,128)} copy(f32[8,4,112,512]{2,1,3,0:T(4,128)} %bitcast.199) | data formatting | bytes 14680064 | tf_op jit(solution)/shard_map/all_to_all | solution.py:128
  595.6 10.6 %bitcast_add_fusion = f32[4,8,112,512]{3,2,1,0:T(8,128)} fusion(f32[4,8,112,512]{3,2,1,0:T(8,128)} %param.18, f32[4,8,112,512]{3,2,1,0:T(8,128)} %bitcast.206), kind=kLoop, calls=%fused_computation.268 | loop fusion | flops 1835008 | bytes 22020096 | tf_op jit(solution)/shard_map/add | solution.py:164
  (117 shorter events, 64.1 us)
Async XLA Ops:
  2.6 5.7 copy-start.8
  2.6 57.7 %collective-permute-start.4 = (f32[2,8,1,512]{3,2,1,0:T(1,128)S(1)}, f32[2,8,1,512]{3,2,1,0:T(1,128)S(1)}, u32[]{:S(2)}, u32[]{:S(2)}) collective-permute-start(f32[2,8,1,512]{3,2,1,0:T(1,128)S(1)} %get-tuple-element.100), channel_id=1, source_target_pairs={{8,0},{16,8},{24,16},{9,1},{17,9},{25,17},{10,2},{18,10},{26,18},{... | collective-permute-start | bytes 98312 | tf_op jit(solution)/shard_map/ppermute | solution.py:22
  3.9 9.0 %copy-start.16 = (s32[512]{0:T(512)S(1)}, s32[512]{0:T(512)}, u32[]{:S(2)}) copy-start(s32[512]{0:T(512)} %param.23) | copy-start | bytes 6148
  4.0 56.3 %collective-permute-start.5 = (f32[2,8,1,512]{3,2,1,0:T(1,128)S(1)}, f32[2,8,1,512]{3,2,1,0:T(1,128)S(1)}, u32[]{:S(2)}, u32[]{:S(2)}) collective-permute-start(f32[2,8,1,512]{3,2,1,0:T(1,128)S(1)} %get-tuple-element.101), channel_id=1, source_target_pairs={{0,8},{8,16},{16,24},{1,9},{9,17},{17,25},{2,10},{10,18},{18,26},{... | collective-permute-start | bytes 98312 | tf_op jit(solution)/shard_map/ppermute | solution.py:20
  9.7 48.9 %collective-permute-start = (f32[2,8,112,1]{2,1,3,0:T(8,128)S(1)}, f32[2,8,112,1]{2,1,3,0:T(8,128)S(1)}, u32[]{:S(2)}, u32[]{:S(2)}) collective-permute-start(f32[2,8,112,1]{2,1,3,0:T(8,128)S(1)} %copy.360), channel_id=1, source_target_pairs={{1,0},{2,1},{3,2},{4,3},{5,4},{6,5},{7,6},{0,7},{9,8},{10,9},{11,1... | collective-permute-start | bytes 21512 | tf_op jit(solution)/shard_map/ppermute | solution.py:22
  10.6 48.4 %collective-permute-start.1 = (f32[2,8,112,1]{2,1,3,0:T(8,128)S(1)}, f32[2,8,112,1]{2,1,3,0:T(8,128)S(1)}, u32[]{:S(2)}, u32[]{:S(2)}) collective-permute-start(f32[2,8,112,1]{2,1,3,0:T(8,128)S(1)} %copy.361), channel_id=1, source_target_pairs={{0,1},{1,2},{2,3},{3,4},{4,5},{5,6},{6,7},{7,0},{8,9},{9,10},{10,1... | collective-permute-start | bytes 21512 | tf_op jit(solution)/shard_map/ppermute | solution.py:20
  44.2 14.3 %copy-start.17 = (f32[8]{0:T(128)S(1)}, f32[8]{0:T(128)}, u32[]{:S(2)}) copy-start(f32[8]{0:T(128)} %param.19) | copy-start | bytes 100
  75.7 1.2 copy-start.11
  77.0 54.2 %collective-permute-start.6 = (f32[1,8,1,512]{3,2,1,0:T(1,128)S(1)}, f32[1,8,1,512]{3,2,1,0:T(1,128)S(1)}, u32[]{:S(2)}, u32[]{:S(2)}) collective-permute-start(f32[1,8,1,512]{3,2,1,0:T(1,128)S(1)} %get-tuple-element.105), channel_id=1, source_target_pairs={{8,0},{16,8},{24,16},{9,1},{17,9},{25,17},{10,2},{18,10},{26,18},{... | collective-permute-start | bytes 49160 | tf_op jit(solution)/shard_map/ppermute | solution.py:22
  78.3 52.9 %collective-permute-start.7 = (f32[1,8,1,512]{3,2,1,0:T(1,128)S(1)}, f32[1,8,1,512]{3,2,1,0:T(1,128)S(1)}, u32[]{:S(2)}, u32[]{:S(2)}) collective-permute-start(f32[1,8,1,512]{3,2,1,0:T(1,128)S(1)} %get-tuple-element.104), channel_id=1, source_target_pairs={{0,8},{8,16},{16,24},{1,9},{9,17},{17,25},{2,10},{10,18},{18,26},{... | collective-permute-start | bytes 49160 | tf_op jit(solution)/shard_map/ppermute | solution.py:20
  119.8 11.5 %copy-start.12 = (f32[1,8,112,512]{3,2,1,0:T(8,128)S(1)}, f32[1,8,112,512]{3,2,1,0:T(8,128)}, u32[]{:S(2)}) copy-start(f32[1,8,112,512]{3,2,1,0:T(8,128)} %copy-done.11) | copy-start | bytes 5505028
  128.0 5.0 copy-start.10
  128.2 15.2 %collective-permute-start.2 = (f32[1,8,112,1]{3,2,1,0:T(8,128)S(1)}, f32[1,8,112,1]{3,2,1,0:T(8,128)S(1)}, u32[]{:S(2)}, u32[]{:S(2)}) collective-permute-start(f32[1,8,112,1]{3,2,1,0:T(8,128)S(1)} %get-tuple-element.106), channel_id=1, source_target_pairs={{1,0},{2,1},{3,2},{4,3},{5,4},{6,5},{7,6},{0,7},{9,8},{10,9},{11,1... | collective-permute-start | bytes 10760 | tf_op jit(solution)/shard_map/ppermute | solution.py:22
  128.3 18.1 %collective-permute-start.3 = (f32[1,8,112,1]{3,2,1,0:T(8,128)S(1)}, f32[1,8,112,1]{3,2,1,0:T(8,128)}, u32[]{:S(2)}, u32[]{:S(2)}) collective-permute-start(f32[1,8,112,1]{3,2,1,0:T(8,128)S(1)} %get-tuple-element.107), channel_id=1, source_target_pairs={{0,1},{1,2},{2,3},{3,4},{4,5},{5,6},{6,7},{7,0},{8,9},{9,10},{10,1... | collective-permute-start | bytes 10760 | tf_op jit(solution)/shard_map/ppermute | solution.py:20
  146.4 4.2 copy-start.9
  146.4 4.2 copy-start.13
  146.4 4.4 copy-start.14
  154.3 8.0 %copy-start.18 = (s32[112]{0:T(128)S(1)}, s32[112]{0:T(128)}, u32[]{:S(2)}) copy-start(s32[112]{0:T(128)} %param.21) | copy-start | bytes 1348
  154.3 8.0 %copy-start.19 = (s32[112]{0:T(128)S(1)}, s32[112]{0:T(128)}, u32[]{:S(2)}) copy-start(s32[112]{0:T(128)} %param.22) | copy-start | bytes 1348
  154.3 163.7 %all-to-all-start = ((f32[32,112,512]{2,1,0:T(8,128)}), f32[32,112,512]{2,1,0:T(8,128)}, u32[]{:S(2)}, u32[]{:S(2)}) async-start(f32[32,112,512]{2,1,0:T(8,128)} %bitcast.204), calls=%async_computation | async-start | bytes 14680064 | tf_op jit(solution)/shard_map/all_to_all | solution.py:124
  322.3 3.9 copy-start.15
  333.0 3.5 copy-start
  336.5 5.3 copy-start.2
  354.2 3.3 copy-start.1
  354.2 3.3 copy-start.3
  408.7 3.5 copy-start.4
  412.2 5.2 copy-start.6
  430.1 3.3 copy-start.5
  430.1 3.3 copy-start.7
where the time goes:
time: 619 us; the launch traced here: 607 us
  waiting for transfers between devices  165 us (27%)
  blocking collectives  161 us (26%)
  matrix products  99.1 us (16%)
  local copies, waits for them, and re-layouts  93.5 us (15%)
  other arithmetic  62.2 us (10%)
  starting transfers between devices  22.6 us (4%)
    all_to_all x1, waiting for transfers between devices, regroup(): lax.all_to_all(merged, 'lon', split_axis=0, concat_axis=2, tiled=True)  154 us
    all_to_all x1, blocking collectives, regroup(): lax.all_to_all(joined, 'lon', split_axis=2, concat_axis=0, tiled=True)  99.6 us
    all_gather x2, blocking collectives, meridional(): circle = lax.all_gather(edge_rows, 'lon', axis=3, tiled=True)  61.5 us
    cond x2, local copies, waits for them, and re-layouts, damp_half(): return lax.cond(active, run_filter, lambda kept: kept, values)  16.6 us
    dot_general x2, matrix products, fourier_damp(): jnp.einsum('brkq,qm->brkm', b_real, large_sin, precision=highest)  15.4 us
  transfers between devices with their start and end apart: 9, of which 3 were waited for; matrix products, arithmetic and copies ran while one was open for 7% of the time, Pallas kernels for 0%

commit v1 on v0

v1 whole, which is shorter than its diff:
```python
import functools
import math

import jax
import jax.numpy as jnp
import numpy as np
from jax import lax
from jax.experimental import pallas as pl
from jax.experimental.pallas import tpu as pltpu
from jax.sharding import PartitionSpec as P

coriolis = 0.3
cos_floor = 0.25
MESH = pl.DeviceIdType.MESH
OUTER = 32
INNER = 128
HALF = OUTER // 2 + 1


def halo_kernel(rows_ref, cols_ref, rows_out, cols_out, circle_ref, lat_send, lat_recv, lon_send, lon_recv, cir_send, cir_recv):
    a, j = lax.axis_index("lat"), lax.axis_index("lon")
    na, nj = lax.axis_size("lat"), lax.axis_size("lon")
    barrier = pltpu.get_barrier_semaphore()

    def greet(t, carry):
        pl.semaphore_signal(barrier, inc=1, device_id=(a, lax.rem(j + t, nj)), device_id_type=MESH)
        return carry

    lax.fori_loop(1, nj, greet, 0)

    for near in (lax.rem(a + 1, na), lax.rem(a + na - 1, na)):
        pl.semaphore_signal(barrier, inc=1, device_id=(near, j), device_id_type=MESH)
    pl.semaphore_wait(barrier, nj + 1)

    pole = jnp.logical_or(a == 0, a == na - 1)
    side = jnp.where(a == 0, 0, 1)

    def lat_copy(s):
        target = a - 1 if s == 0 else a + 1
        return pltpu.make_async_remote_copy(
            rows_ref.at[s], rows_out.at[1 - s], lat_send.at[s], lat_recv.at[1 - s],
            device_id=(target, j), device_id_type=MESH)

    def lon_copy(s):
        target = lax.rem(j + (nj - 1 if s == 0 else 1), nj)
        return pltpu.make_async_remote_copy(
            cols_ref.at[s], cols_out.at[1 - s], lon_send.at[s], lon_recv.at[1 - s],
            device_id=(a, target), device_id_type=MESH)

    def circle_copy(t):
        return pltpu.make_async_remote_copy(
            rows_ref.at[side], circle_ref.at[j], cir_send.at[t], cir_recv.at[j],
            device_id=(a, lax.rem(j + t, nj)), device_id_type=MESH)

    def circle_wait(t):
        source = lax.rem(j + t, nj)
        return pltpu.make_async_remote_copy(
            rows_ref.at[side], circle_ref.at[source], cir_send.at[t], cir_recv.at[source],
            device_id=(a, source), device_id_type=MESH)

    own = pltpu.make_async_copy(rows_ref.at[side], circle_ref.at[j], cir_recv.at[j])

    @pl.when(pole)
    def _():
        lax.fori_loop(1, nj, lambda t, c: (circle_copy(t).start(), c)[1], 0)
        own.start()

    lon_copy(0).start()
    lon_copy(1).start()

    @pl.when(a > 0)
    def _():
        lat_copy(0).start()

    @pl.when(a < na - 1)
    def _():
        lat_copy(1).start()

    lon_copy(0).wait()
    lon_copy(1).wait()

    @pl.when(a > 0)
    def _():
        lat_copy(0).wait_send()
        lat_copy(1).wait_recv()

    @pl.when(a < na - 1)
    def _():
        lat_copy(1).wait_send()
        lat_copy(0).wait_recv()

    @pl.when(pole)
    def _():
        def finish(t, carry):
            circle_copy(t).wait_send()
            circle_wait(t).wait_recv()
            return carry

        lax.fori_loop(1, nj, finish, 0)
        own.wait()


def exchange_halos(rows, cols):
    nj = lax.axis_size("lon")
    vmem = pl.BlockSpec(memory_space=pltpu.VMEM)
    dma = pltpu.SemaphoreType.DMA
    return pl.pallas_call(
        halo_kernel,
        out_shape=(
            jax.ShapeDtypeStruct(rows.shape, jnp.float32),
            jax.ShapeDtypeStruct(cols.shape, jnp.float32),
            jax.ShapeDtypeStruct((nj,) + rows.shape[1:], jnp.float32),
        ),
        in_specs=[vmem, vmem],
        out_specs=(vmem, vmem, vmem),
        scratch_shapes=[dma((2,)), dma((2,)), dma((2,)), dma((2,)), dma((nj,)), dma((nj,))],
        compiler_params=pltpu.CompilerParams(collective_id=0, has_side_effects=True),
        name="halos",
    )(rows, cols)


def real_forward(values):
    n = len(values)
    if n == 1:
        return [(values[0], None)]
    if n == 2:
        return [(values[0] + values[1], None), (values[0] - values[1], None)]
    even = real_forward(values[0::2])
    odd = real_forward(values[1::2])
    half = n // 2
    out = [None] * (half + 1)
    for k in range(half // 2 + 1):
        er, ei = even[k]
        orr, oi = odd[k]
        if k == 0:
            out[0] = (er + orr, None)
            out[half] = (er - orr, None)
            continue
        c, s = math.cos(2 * math.pi * k / n), math.sin(2 * math.pi * k / n)
        if k == half // 2:
            out[k] = (er, -orr)
            continue
        if oi is None:
            tr, ti = c * orr, -s * orr
        else:
            tr, ti = c * orr + s * oi, c * oi - s * orr
        eii = 0.0 if ei is None else ei
        out[k] = (er + tr, eii + ti)
        out[half - k] = (er - tr, ti - eii)
    return out


def real_backward(spec):
    n = 2 * (len(spec) - 1)
    if n == 2:
        return [spec[0][0] + spec[1][0], spec[0][0] - spec[1][0]]
    half = n // 2
    even, odd = [], []
    for k in range(half // 2 + 1):
        xr, xi = spec[k]
        yr, yi = spec[half - k]
        if k == 0:
            even.append((xr + yr, None))
            odd.append((xr - yr, None))
            continue
        if k == half // 2:
            even.append((2.0 * xr, None))
            odd.append((-2.0 * xi, None))
            continue
        c, s = math.cos(2 * math.pi * k / n), math.sin(2 * math.pi * k / n)
        dr, di = xr - yr, xi + yi
        even.append((xr + yr, xi - yi))
        odd.append((c * dr - s * di, c * di + s * dr))
    out = [None] * n
    out[0::2] = real_backward(even)
    out[1::2] = real_backward(odd)
    return out


def split(x):
    high = x.astype(jnp.bfloat16)
    return high, (x - high.astype(jnp.float32)).astype(jnp.bfloat16)


def dot3(x, w_ref):
    high, low = split(x)
    dot = functools.partial(jnp.dot, preferred_element_type=jnp.float32)
    return dot(high, w_ref[0]) + (dot(low, w_ref[0]) + dot(high, w_ref[1]))


def circle_kernel(upd, parts, inc_ref, damp_ref, twid_ref, fwd_ref, bwd_ref, out_ref, recv, done, spec, send1, recv1, send2, recv2):
    a, j = lax.axis_index("lat"), lax.axis_index("lon")
    na, nj = lax.axis_size("lat"), lax.axis_size("lon")
    quarter = na // 4
    low = a < na // 2
    active = jnp.logical_or(a < quarter, a >= na - quarter)
    mirror = jnp.where(low, 2 * quarter - 1 - a, 2 * na - 2 * quarter - 1 - a)
    source_lat = jnp.where(active, a, mirror)
    helper_lat = jnp.where(active, mirror, a)
    mine = jnp.where(active, j, nj + j)
    count = 2 * nj
    part_rows = recv.shape[2]
    width = recv.shape[3]

    def place(d):
        return (jnp.where(d < nj, source_lat, helper_lat), lax.rem(d, nj))

    def unit(ref, d, c):
        u = d * upd + c
        r = pl.multiple_of(lax.rem(u, parts) * part_rows, 8)
        return ref.at[u // parts, pl.ds(r, part_rows), :]

    barrier = pltpu.get_barrier_semaphore()

    def greet(t, carry):
        pl.semaphore_signal(barrier, inc=1, device_id=place(lax.rem(mine + t, count)), device_id_type=MESH)
        return carry

    lax.fori_loop(1, count, greet, 0)
    pl.semaphore_wait(barrier, count - 1)

    def out_copy(c, t):
        d = lax.rem(mine + t, count)
        return pltpu.make_async_remote_copy(
            unit(inc_ref, d, c), recv.at[c, j], send1.at[c, t], recv1.at[c, j],
            device_id=place(d), device_id_type=MESH)

    def out_own(c):
        return pltpu.make_async_copy(unit(inc_ref, mine, c), recv.at[c, j], recv1.at[c, j])

    def in_wait(c, s):
        return pltpu.make_async_remote_copy(
            unit(inc_ref, mine, c), recv.at[c, s], send1.at[c, 0], recv1.at[c, s],
            device_id=(source_lat, s), device_id_type=MESH)

    def back_copy(c, s):
        return pltpu.make_async_remote_copy(
            done.at[c, s], unit(out_ref, mine, c), send2.at[c, s], recv2.at[c, mine],
            device_id=(source_lat, s), device_id_type=MESH)

    def back_own(c):
        return pltpu.make_async_copy(done.at[c, j], unit(out_ref, mine, c), recv2.at[c, mine])

    def back_wait(c, d):
        return pltpu.make_async_remote_copy(
            done.at[c, j], unit(out_ref, d, c), send2.at[c, j], recv2.at[c, d],
            device_id=place(d), device_id_type=MESH)

    @pl.when(active)
    def _():
        def launch(c, carry):
            lax.fori_loop(1, count, lambda t, k: (out_copy(c, t).start(), k)[1], 0)
            out_own(c).start()
            return carry

        lax.fori_loop(0, upd, launch, 0)

    tiles = part_rows // 8
    per = width // INNER

    def handle(c, carry):
        def arrive(t, k):
            in_wait(c, lax.rem(j + t, nj)).wait_recv()
            return k

        lax.fori_loop(1, nj, arrive, 0)

        @pl.when(active)
        def _():
            out_own(c).wait()

        @pl.when(jnp.logical_not(active))
        def _():
            in_wait(c, j).wait_recv()

        def analyse(i, k):
            r = pl.ds(pl.multiple_of(i * 8, 8), 8)
            values = [
                recv[c, p // per, r, (p % per) * INNER : (p % per + 1) * INNER] for p in range(OUTER)
            ]
            for q, (re, im) in enumerate(real_forward(values)):
                cos, sin = twid_ref[0, q : q + 1, :], twid_ref[1, q : q + 1, :]
                if im is None:
                    spec[q, r, :INNER] = re * cos
                    spec[q, r, INNER:] = -re * sin
                else:
                    spec[q, r, :INNER] = re * cos + im * sin
                    spec[q, r, INNER:] = im * cos - re * sin
            return k

        lax.fori_loop(0, tiles, analyse, 0)
        h = lax.rem(mine * upd + c, parts)
        full = dot3(spec[...].reshape(HALF * part_rows, 2 * INNER), fwd_ref)
        weight = damp_ref[h].reshape(HALF * part_rows, INNER)
        full = full * jnp.concatenate([weight, weight], axis=1)
        spec[...] = dot3(full, bwd_ref).reshape(HALF, part_rows, 2 * INNER)

        def synthesise(i, k):
            r = pl.ds(pl.multiple_of(i * 8, 8), 8)
            waves = []
            for q in range(HALF):
                cos, sin = twid_ref[0, q : q + 1, :], twid_ref[1, q : q + 1, :]
                re, im = spec[q, r, :INNER], spec[q, r, INNER:]
                waves.append((re * cos - im * sin, im * cos + re * sin))
            for p, value in enumerate(real_backward(waves)):
                done[c, p // per, r, (p % per) * INNER : (p % per + 1) * INNER] = value
            return k

        lax.fori_loop(0, tiles, synthesise, 0)
        lax.fori_loop(1, nj, lambda t, k: (back_copy(c, lax.rem(j + t, nj)).start(), k)[1], 0)

        @pl.when(active)
        def _():
            back_own(c).start()

        @pl.when(jnp.logical_not(active))
        def _():
            back_copy(c, j).start()

        return carry

    lax.fori_loop(0, upd, handle, 0)

    def settle(c, carry):
        lax.fori_loop(1, nj, lambda t, k: (back_copy(c, lax.rem(j + t, nj)).wait_send(), k)[1], 0)

        @pl.when(active)
        def _():
            def finish(t, k):
                out_copy(c, t).wait_send()
                back_wait(c, lax.rem(mine + t, count)).wait_recv()
                return k

            lax.fori_loop(1, count, finish, 0)
            back_own(c).wait()

        @pl.when(jnp.logical_not(active))
        def _():
            back_copy(c, j).wait_send()

        return carry

    lax.fori_loop(0, upd, settle, 0)


def constants():
    k = np.arange(HALF)[:, None]
    q = np.arange(INNER)[None, :]
    turn = 2 * np.pi * (k * q) / (OUTER * INNER)
    twiddle = np.stack([np.cos(turn), np.sin(turn)]).astype(np.float32)
    turn = 2 * np.pi * ((q.T * q) % INNER) / INNER
    cos, sin = np.cos(turn), np.sin(turn)
    forward = np.block([[cos, -sin], [sin, cos]])

    def pair(m):
        high = m.astype(jnp.bfloat16)
        return np.stack([high, (m - high.astype(np.float64)).astype(jnp.bfloat16)])

    return jnp.asarray(twiddle), jnp.asarray(pair(forward)), jnp.asarray(pair(forward.T))


def filter_circles(inc, weights, parts):
    nj = lax.axis_size("lon")
    stacks, rows, width = inc.shape
    upd = stacks * parts // (2 * nj)
    part_rows = rows // parts
    vmem = pl.BlockSpec(memory_space=pltpu.VMEM)
    hbm = pl.BlockSpec(memory_space=pl.ANY)
    dma = pltpu.SemaphoreType.DMA
    twiddle, forward, backward = constants()
    return pl.pallas_call(
        functools.partial(circle_kernel, upd, parts),
        out_shape=jax.ShapeDtypeStruct(inc.shape, jnp.float32),
        in_specs=[hbm, vmem, vmem, vmem, vmem],
        out_specs=hbm,
        scratch_shapes=[
            pltpu.VMEM((upd, nj, part_rows, width), jnp.float32),
            pltpu.VMEM((upd, nj, part_rows, width), jnp.float32),
            pltpu.VMEM((HALF, part_rows, 2 * INNER), jnp.float32),
            dma((upd, 2 * nj)),
            dma((upd, nj)),
            dma((upd, nj)),
            dma((upd, 2 * nj)),
        ],
        compiler_params=pltpu.CompilerParams(
            collective_id=1, has_side_effects=True, vmem_limit_bytes=40 * 1024 * 1024
        ),
        name="circles",
    )(inc, weights, twiddle, forward, backward)


def per_device(state, level_courant, damp_table, row_flag, row_table, partner):
    fields_n, levels_n, rows_n, cols_n = state.shape
    na = lax.axis_size("lat")
    a = lax.axis_index("lat")
    whole_rows = rows_n * na

    def geometry(row_pos):
        latitude = -jnp.pi / 2 + jnp.pi * (row_pos.astype(jnp.float32) + 0.5) / whole_rows
        return jnp.cos(latitude), jnp.sin(latitude)

    first_row = a * rows_n
    cos1, sin1 = geometry(first_row + jnp.arange(rows_n, dtype=jnp.int32))
    cos_lat, sin_lat = cos1[:, None], sin1[:, None]
    metric1 = 1.0 / jnp.maximum(cos1, cos_floor)
    metric = metric1[:, None]
    c1 = level_courant[:, None]
    courant = level_courant[:, None, None]
    p, u, v, th = state[0], state[1], state[2], state[3]
    meet = jnp.broadcast_to(partner.astype(jnp.float32)[None, :], (8, cols_n))

    def row_pack(outer, inner):
        return jnp.concatenate(
            [p[:, outer], p[:, inner], u[:, outer], v[:, outer], th[:, outer], meet], axis=0
        )

    def col_pack(outer, inner):
        return jnp.concatenate(
            [p[:, :, outer], p[:, :, inner], u[:, :, outer], v[:, :, outer], th[:, :, outer]], axis=0
        )

    rows = jnp.stack([row_pack(0, 1), row_pack(rows_n - 1, rows_n - 2)])
    cols = jnp.stack([col_pack(0, 1), col_pack(cols_n - 1, cols_n - 2)])
    rows_in, cols_in, circle = exchange_halos(rows, cols)

    def fields_of(pack):
        return [pack[8 * k : 8 * k + 8] for k in range(5)]

    at_south, at_north = a == 0, a == na - 1
    whole = jnp.transpose(circle, (1, 0, 2)).reshape(circle.shape[1], -1)
    met = jnp.take(whole, partner, axis=1)
    twice = jnp.clip(met[40].astype(jnp.int32), 0, whole.shape[1] - 1)
    p_twice = jnp.take(whole[:8], twice, axis=1)
    p_met, p_met_in, u_met, v_met, th_met = fields_of(met)
    cos_end = jnp.where(at_south, cos1[0], cos1[-1])
    sin_end = jnp.where(at_south, sin1[0], sin1[-1])
    rise = jnp.where(at_south, p_met_in - p_twice, p_twice - p_met_in)
    flux_met = -(v_met + (-c1 * rise * 0.5 - coriolis * sin_end * u_met)) * cos_end

    ps, ps2, us, vs, ths = fields_of(rows_in[0])
    pn, pn2, un, vn, thn = fields_of(rows_in[1])
    cos_s, sin_s = geometry(first_row - 1)
    cos_n, sin_n = geometry(first_row + rows_n)
    flux_s = (vs + (-c1 * (p[:, 0] - ps2) * 0.5 - coriolis * sin_s * us)) * cos_s
    flux_n = (vn + (-c1 * (pn2 - p[:, -1]) * 0.5 - coriolis * sin_n * un)) * cos_n
    ps, ths, flux_s = (jnp.where(at_south, m, o) for m, o in ((p_met, ps), (th_met, ths), (flux_met, flux_s)))
    pn, thn, flux_n = (jnp.where(at_north, m, o) for m, o in ((p_met, pn), (th_met, thn), (flux_met, flux_n)))

    pw, pw2, uw, vw, thw = fields_of(cols_in[0])
    pe, pe2, ue, ve, the = fields_of(cols_in[1])
    u_west = uw + (-c1 * metric1 * (p[:, :, 0] - pw2) * 0.5 + coriolis * sin1 * vw)
    u_east = ue + (-c1 * metric1 * (pe2 - p[:, :, -1]) * 0.5 + coriolis * sin1 * ve)

    def zonal(f, west, east):
        return jnp.concatenate([f[:, :, 1:], east[:, :, None]], axis=2) - jnp.concatenate(
            [west[:, :, None], f[:, :, :-1]], axis=2
        )

    def merid(f, south, north):
        return jnp.concatenate([f[:, 1:], north[:, None, :]], axis=1) - jnp.concatenate(
            [south[:, None, :], f[:, :-1]], axis=1
        )

    tend_u = -courant * metric * zonal(p, pw, pe) * 0.5 + coriolis * sin_lat * v
    tend_v = -courant * merid(p, ps, pn) * 0.5 - coriolis * sin_lat * u
    u_new = u + tend_u
    v_new = v + tend_v
    flux = v_new * cos_lat
    divergence = courant * metric * (zonal(u_new, u_west, u_east) * 0.5 + merid(flux, flux_s, flux_n) * 0.5)
    tend_t = -courant * metric * u_new * zonal(th, thw, the) * 0.5 - courant * v_new * merid(th, ths, thn) * 0.5
    inc = jnp.concatenate([-divergence, tend_u, tend_v, tend_t])

    quarter = na // 4
    pairs = [(i, 2 * quarter - 1 - i if i < na // 2 else 2 * na - 2 * quarter - 1 - i) for i in range(na)]
    active = (a < quarter) | (a >= na - quarter)
    table = jnp.where(active, row_table, lax.ppermute(row_table, "lat", pairs))
    parts = 2
    count = damp_table.shape[0]
    length = OUTER * INNER
    full = jnp.concatenate(
        [jnp.ones((count, 1), jnp.float32), damp_table, jnp.flip(damp_table[:, :-1], axis=1)], axis=1
    )
    grid = jnp.transpose(full.reshape(count, INNER, OUTER), (0, 2, 1))[:, :HALF] * (1.0 / length)
    pick = (table[:, None] == jnp.arange(count, dtype=jnp.int32)[None, :]).astype(jnp.float32)
    weights = jnp.einsum(
        "hrt,tkm->hkrm", pick.reshape(parts, rows_n // parts, count), grid, precision=lax.Precision.HIGHEST
    )
    smooth = filter_circles(inc, weights, parts)
    chosen = (active & (row_flag == 1))[None, :, None]
    result = state.reshape(inc.shape) + jnp.where(chosen, smooth, inc)
    return result.reshape(state.shape)


def solution(mesh):
    placed = (P(None, None, "lat", "lon"), P(), P(), P("lat"), P("lat"), P("lon"))
    return jax.shard_map(
        per_device,
        mesh=mesh,
        in_specs=placed,
        out_specs=P(None, None, "lat", "lon"),
        check_vma=False,
    )
```

time: 619 us -> 276 us (0.45); the launches traced: 607 us -> 276 us
  Pallas kernels: 0 us -> 183 us
  waiting for transfers between devices: 165 us -> 0.01 us
  blocking collectives: 161 us -> 0 us
  matrix products: 99.1 us -> 0.59 us
  local copies, waits for them, and re-layouts: 93.5 us -> 57.3 us
  other arithmetic: 62.2 us -> 31.3 us
  starting transfers between devices: 22.6 us -> 0.01 us
    pallas_call x0 -> x2, Pallas kernels: none -> 183 us  [the longest x1 166 us: filter_circles(): pl.pallas_call(functools.partial(circle_kernel, upd, parts), out_shape=ja...]
    all_to_all x1 -> x0, waiting for transfers between devices: 154 us -> none  [regroup(): lax.all_to_all(merged, 'lon', split_axis=0, concat_axis=2, tiled=True)]
    all_to_all x1 -> x0, blocking collectives: 99.6 us -> none  [regroup(): lax.all_to_all(joined, 'lon', split_axis=2, concat_axis=0, tiled=True)]
    dot_general x26 -> x1, matrix products: 99.1 us -> 0.59 us  [per_device(): jnp.einsum('hrt,tkm->hkrm', pick.reshape(parts, rows_n // parts, count),...]
    all_gather x2 -> x0, blocking collectives: 61.5 us -> none  [meridional(): circle = lax.all_gather(edge_rows, 'lon', axis=3, tiled=True)]
    cond x24 -> x0, local copies, waits for them, and re-layouts: 25.5 us -> none  [the longest x2 16.6 us: damp_half(): return lax.cond(active, run_filter, lambda kept: kept, values)]
    slice x9 -> x27, local copies, waits for them, and re-layouts: 6.72 us -> 29.5 us  [the longest x3 7.44 us: zonal(): f[:, :, :-1]]
    ppermute x8 -> x1, starting transfers between devices: 14.6 us -> 0.01 us  [per_device(): table = jnp.where(active, row_table, lax.ppermute(row_table, 'lat', pairs))]
  transfers between devices with their start and end apart: 9 -> 1, of which waited for: 3 -> 0; matrix products, arithmetic and copies ran while one was open for 7% -> 28% of each run, Pallas kernels for 0% -> 6%
where the time goes in v1:
time: 276 us
  Pallas kernels  183 us (66%)
  local copies, waits for them, and re-layouts  57.3 us (21%)
  other arithmetic  31.3 us (11%)
  between operations  3.57 us (1%)
    pallas_call x1, Pallas kernels, filter_circles(): pl.pallas_call(functools.partial(circle_kernel, upd, parts), out_shape=ja...  166 us
    pallas_call x1, Pallas kernels, exchange_halos(): pl.pallas_call(halo_kernel, out_shape=(jax.ShapeDtypeStruct(rows.shape, j...  16.7 us
    squeeze x2, local copies, waits for them, and re-layouts, per_device(): p, u, v, th = (state[0], state[1], state[2], state[3])  7.87 us
    slice x3, local copies, waits for them, and re-layouts, zonal(): f[:, :, :-1]  7.44 us
    sub x1, other arithmetic, per_device(): -courant * metric * u_new * zonal(th, thw, the) * 0.5  7.39 us
    add x1, other arithmetic, per_device(): result = state.reshape(inc.shape) + jnp.where(chosen, smooth, inc)  7.06 us
    slice x3, local copies, waits for them, and re-layouts, merid(): f[:, :-1]  6.84 us
  transfers between devices with their start and end apart: 1, of which 0 were waited for; matrix products, arithmetic and copies ran while one was open for 28% of the time, Pallas kernels for 6%

profile of v1, /device:TPU:10, one launch (start us, length us, event | category | flops | bytes accessed | tf_op | source)
XLA Modules:
  0.0 275.5 jit_solution(3626470602526320612)
XLA Ops:
  0.0 4.5 %slice_bitcast_fusion = (f32[8,112,512]{2,1,0:T(8,128)S(1)}, f32[1,8,112,512]{3,2,1,0:T(8,128)S(1)}, f32[1,8,112,512]{3,2,1,0:T(8,128)S(1)}, f32[8,112,512]{2,1,0:T(8,128)S(1)}) fusion(f32[4,8,112,512]{3,2,1,0:T(8,128)} %param.9), kind=kLoop, calls=%fused_computation.27 | loop fusion | bytes 14680064 | tf_op jit(solution)/shard_map/squeeze | solution.py:409
  4.5 3.4 %copy_bitcast_fusion = (f32[8,112,512]{2,0,1:T(8,128)S(1)}, f32[8,112,512]{2,0,1:T(8,128)}) fusion(f32[1,8,112,512]{3,2,1,0:T(8,128)S(1)} %get-tuple-element.23, f32[1,8,112,512]{3,2,1,0:T(8,128)S(1)} %get-tuple-element.22), kind=kLoop, calls=%fused_computation.22 | loop fusion | bytes 7340032 | tf_op jit(solution)/shard_map/squeeze | solution.py:409
  7.9 1.2 fusion.61
  9.2 0.9 slice_reduce_fusion.2
  10.1 2.5 fusion.56
  12.6 1.2 copy.446
  14.0 2.1 fusion.60
  16.1 1.2 copy.448
  17.9 0.8 constant_dynamic-update-slice_fusion.3
  18.8 0.7 pad_maximum_fusion.1.rows_ref
  19.5 0.6 pad_maximum_fusion.2.cols_ref
  20.1 16.7 %halos.1 = (f32[2,48,512]{2,1,0:T(8,128)}, f32[2,40,112]{2,1,0:T(8,128)}, f32[8,48,512]{2,1,0:T(8,128)}) custom-call(f32[2,48,512]{2,1,0:T(8,128)} %pad_maximum_fusion.1.rows_ref, f32[2,40,112]{2,1,0:T(8,128)} %pad_maximum_fusion.2.cols_ref), custom_call_target="tpu_custom_call" | custom-call | tf_op jit(solution)/shard_map/halos/pallas_call | solution.py:107
  36.9 3.1 %copy.482 = f32[48,8,512]{0,2,1:T(8,128)} copy(f32[48,8,512]{2,0,1:T(8,128)} %bitcast.210) | data formatting | bytes 1572864 | tf_op jit(solution)/shard_map/reshape | solution.py:430
  39.9 0.9 slice.405
  40.9 2.6 gather_fusion
  44.1 2.4 fusion.57
  46.5 2.2 fusion.58
  48.7 2.4 fusion.59
  51.9 1.0 copy.462
  52.9 1.0 copy.463
  53.9 1.0 copy.464
  55.0 1.7 fusion.18
  56.8 0.9 copy.465
  58.2 1.9 copy.471
  60.1 3.2 %gather_fusion.1 = f32[512,8]{1,0:T(8,128)} fusion(f32[8,4096]{0,1:T(8,128)} %copy.471, s32[1024]{0:T(1024)S(1)} %pad_clamp_fusion), kind=kCustom, calls=%fused_computation.1 | custom fusion | bytes 34816 | tf_op jit(solution)/shard_map/jit(_take)/gather | solution.py:433
  63.3 1.0 copy.472
  64.4 0.6 fusion.65
  65.0 0.6 fusion.64
  68.2 0.9 fusion.31
  69.1 0.9 fusion.43
  70.0 1.0 copy.475
  71.0 1.0 copy.476
  72.0 2.9 %maximum_subtract_fusion = f32[8,112,512]{2,0,1:T(8,128)S(1)} fusion(f32[8,112,1]{2,0,1:T(8,128)S(1)} %copy.452, f32[8,112,511]{2,0,1:T(8,128)} %get-tuple-element.33, f32[8,112,511]{2,0,1:T(8,128)} %get-tuple-element.32, f32[8,112,1]{2,0,1:T(8,128)S(1)} %copy.453), kind=kLoop, calls=%fused_computation.4 | loop fusion | flops 1376256 | bytes 5505024 | tf_op jit(solution)/shard_map/sub | solution.py:455
  75.1 0.5 copy-done.19
  75.7 1.2 fusion.5
  77.2 0.6 copy-done.15
  77.8 0.6 copy-done.16
  78.3 0.5 copy-done.17
  78.8 7.4 %fusion.8 = (f32[8,112,512]{2,1,0:T(8,128)}, f32[8,112,512]{2,1,0:T(8,128)S(1)}, f32[8,112,512]{2,1,0:T(8,128)}, f32[8,112,512]{2,1,0:T(8,128)S(1)}, f32[8,112,512]{2,1,0:T(8,128)}) fusion(f32[8,112,1]{2,1,0:T(8,128)S(1)} %copy-done.21, f32[8,112,511]{2,1,0:T(8,128)S(1)} %copy-done.17, f32[8,112,511]{2,1,0:T(8,128)S(1)} %copy-done.16, ...), kind=kLoop, calls=%fused_computation.17 | loop fusion | flops 9175040 | bytes 23859616 | tf_op jit(solution)/shard_map/sub | solution.py:470
  86.2 2.2 fusion.54
  88.5 2.5 fusion.55
  91.1 4.3 %fusion.2 = f32[8,112,512]{2,1,0:T(8,128)S(1)} fusion(f32[8,112,1]{2,1,0:T(8,128)S(1)} %copy.461, f32[8,112,511]{2,1,0:T(8,128)} %get-tuple-element.30, f32[8,112,511]{2,1,0:T(8,128)} %get-tuple-element.29, f32[8,112,1]{2,1,0:T(8,128)S(1)} %copy-done.20, f32[8,1,512]{2,1,0:T(1,128)S(1)} %copy.473, f32[8,111,512]{2,1,0:T(8,128)} %get-tuple-element.28, ...), kind=kLoop, calls=%fused_computation.8 | loop fusion | flops 4128768 | bytes 9178624 | tf_op jit(solution)/shard_map/neg | solution.py:471
  95.4 0.4 copy-done.9
  95.8 3.5 %pad_maximum_fusion.inc_ref = f32[32,112,512]{2,1,0:T(8,128)} fusion(f32[8,112,512]{2,1,0:T(8,128)S(1)} %copy-done.5, f32[8,112,512]{2,1,0:T(8,128)S(1)} %copy-done.9, f32[8,112,512]{2,1,0:T(8,128)S(1)} %copy-done.7, f32[8,112,512]{2,1,0:T(8,128)S(1)} %fusion.2), kind=kLoop, calls=%fused_computation.2 | loop fusion | flops 5505024 | bytes 14680064 | tf_op jit(solution)/shard_map/concatenate | solution.py:471
  99.3 1.3 reverse
  101.8 0.6 convolution_bitcast_fusion.damp_ref
  102.4 166.0 %circles.1 = f32[32,112,512]{2,1,0:T(8,128)S(1)} custom-call(f32[32,112,512]{2,1,0:T(8,128)} %pad_maximum_fusion.inc_ref, f32[2,17,56,128]{3,2,1,0:T(8,128)S(1)} %convolution_bitcast_fusion.damp_ref, f32[2,17,128]{2,1,0:T(8,128)S(1)} %copy-done.2, bf16[2,256,256]{2,1,0:T(8,128)(2,1)S(1)} %copy-done, bf16[2,256,256]{2,1,0:T(8,128)(2,1)S(1)} %copy-done.1), custom_call_target="tpu_custom_call" | custom-call | tf_op jit(solution)/shard_map/circles/pallas_call | solution.py:371
  268.4 7.1 %bitcast_add_fusion = f32[32,112,512]{2,1,0:T(8,128)} fusion(f32[4,8,112,512]{3,2,1,0:T(8,128)} %param.9, f32[32,112,512]{2,1,0:T(8,128)S(1)} %circles.1, pred[112]{0:T(512)(128)(4,1)S(1)} %compare_and_fusion.2, f32[8,112,512]{2,1,0:T(8,128)S(1)} %copy-done.6, f32[8,112,512]{2,1,0:T(8,128)S(1)} %copy-done.10, f32[8,112,512]{2,1,0:T(8,128)S(1)} %copy-done.8, ...), kind=kLoop, calls=%fused_computation.3 | loop fusion | flops 9175040 | bytes 29360240 | tf_op jit(solution)/shard_map/add | solution.py:490
  (109 shorter events, 4.4 us)
Async XLA Ops:
  0.0 101.6 %collective-permute-start = (s32[112]{0:T(128)}, s32[112]{0:T(128)S(1)}, u32[]{:S(2)}, u32[]{:S(2)}) collective-permute-start(s32[112]{0:T(128)} %param.13), channel_id=1, source_target_pairs={{0,8},{8,0},{16,24},{24,16},{1,9},{9,1},{17,25},{25,17},{2,10},{10... | collective-permute-start | bytes 1352 | tf_op jit(solution)/shard_map/ppermute | solution.py:476
  4.5 3.4 %copy-start.11 = (f32[1,8,112,512]{3,2,1,0:T(8,128)}, f32[1,8,112,512]{3,2,1,0:T(8,128)S(1)}, u32[]{:S(2)}) copy-start(f32[1,8,112,512]{3,2,1,0:T(8,128)S(1)} %get-tuple-element.22) | copy-start | bytes 5505028
  4.5 4.6 %copy-start.3 = (f32[8,112,512]{2,1,0:T(8,128)}, f32[8,112,512]{2,1,0:T(8,128)S(1)}, u32[]{:S(2)}) copy-start(f32[8,112,512]{2,1,0:T(8,128)S(1)} %get-tuple-element.21) | copy-start | bytes 5505028
  10.1 2.5 copy-start.25
  44.1 2.4 copy-start.4
  48.7 2.5 copy-start.24
  51.1 3.7 %copy-start.26 = (f32[8]{0:T(128)S(1)}, f32[8]{0:T(128)}, u32[]{:S(2)}) copy-start(f32[8]{0:T(128)} %param.10) | copy-start | bytes 100
  72.0 2.9 %copy-start.12 = (f32[1,8,112,512]{3,2,1,0:T(8,128)S(1)}, f32[1,8,112,512]{3,2,1,0:T(8,128)}, u32[]{:S(2)}) copy-start(f32[1,8,112,512]{3,2,1,0:T(8,128)} %copy-done.11) | copy-start | bytes 5505028
  72.0 3.1 %copy-start.18 = (f32[8,111,512]{2,0,1:T(8,128)S(1)}, f32[8,111,512]{2,0,1:T(8,128)}, u32[]{:S(2)}) copy-start(f32[8,111,512]{2,0,1:T(8,128)} %get-tuple-element.34) | copy-start | bytes 5455876
  72.0 3.7 %copy-start.19 = (f32[8,111,512]{2,0,1:T(8,128)S(1)}, f32[8,111,512]{2,0,1:T(8,128)}, u32[]{:S(2)}) copy-start(f32[8,111,512]{2,0,1:T(8,128)} %get-tuple-element.35) | copy-start | bytes 5455876
  72.0 4.9 %copy-start.21 = (f32[8,112,1]{2,1,0:T(8,128)S(1)}, f32[8,112,1]{2,1,0:T(8,128)}, u32[]{:S(2)}) copy-start(f32[8,112,1]{2,1,0:T(8,128)} %copy.475) | copy-start | bytes 10756
  72.0 4.9 %copy-start.22 = (f32[8,112,1]{2,1,0:T(8,128)S(1)}, f32[8,112,1]{2,1,0:T(8,128)}, u32[]{:S(2)}) copy-start(f32[8,112,1]{2,1,0:T(8,128)} %copy.476) | copy-start | bytes 10756
  75.7 1.5 copy-start.14
  75.7 2.1 copy-start.15
  75.7 2.6 copy-start.16
  75.7 3.2 %copy-start.17 = (f32[8,112,511]{2,1,0:T(8,128)S(1)}, f32[8,112,511]{2,1,0:T(8,128)}, u32[]{:S(2)}) copy-start(f32[8,112,511]{2,1,0:T(8,128)} %get-tuple-element.39) | copy-start | bytes 5494276
  88.5 2.5 copy-start.28
  88.5 2.6 copy-start.20
  91.0 4.4 %copy-start.5 = (f32[8,112,512]{2,1,0:T(8,128)S(1)}, f32[8,112,512]{2,1,0:T(8,128)}, u32[]{:S(2)}) copy-start(f32[8,112,512]{2,1,0:T(8,128)} %get-tuple-element.17) | copy-start | bytes 5505028
  91.1 4.4 %copy-start.7 = (f32[8,112,512]{2,1,0:T(8,128)S(1)}, f32[8,112,512]{2,1,0:T(8,128)}, u32[]{:S(2)}) copy-start(f32[8,112,512]{2,1,0:T(8,128)} %get-tuple-element.19) | copy-start | bytes 5505028
  91.1 4.8 %copy-start.9 = (f32[8,112,512]{2,1,0:T(8,128)S(1)}, f32[8,112,512]{2,1,0:T(8,128)}, u32[]{:S(2)}) copy-start(f32[8,112,512]{2,1,0:T(8,128)} %get-tuple-element.31) | copy-start | bytes 5505028
  95.4 3.9 %copy-start.13 = (f32[8,112,512]{2,1,0:T(8,128)}, f32[8,112,512]{2,1,0:T(8,128)S(1)}, u32[]{:S(2)}) copy-start(f32[8,112,512]{2,1,0:T(8,128)S(1)} %fusion.2) | copy-start | bytes 5505028
  95.8 3.5 %copy-start.23 = (f32[16,2048]{1,0:T(8,128)S(1)}, f32[16,2048]{1,0:T(8,128)}, u32[]{:S(2)}) copy-start(f32[16,2048]{1,0:T(8,128)} %param.11) | copy-start | bytes 393220
  99.3 2.3 copy-start.27
  100.9 1.4 copy-start
  100.9 1.4 copy-start.1
  100.9 1.4 copy-start.2
  102.4 166.0 %copy-start.6 = (f32[8,112,512]{2,1,0:T(8,128)S(1)}, f32[8,112,512]{2,1,0:T(8,128)}, u32[]{:S(2)}) copy-start(f32[8,112,512]{2,1,0:T(8,128)} %get-tuple-element.17) | copy-start | bytes 5505028
  102.4 166.0 %copy-start.8 = (f32[8,112,512]{2,1,0:T(8,128)S(1)}, f32[8,112,512]{2,1,0:T(8,128)}, u32[]{:S(2)}) copy-start(f32[8,112,512]{2,1,0:T(8,128)} %get-tuple-element.19) | copy-start | bytes 5505028
  102.4 166.0 %copy-start.10 = (f32[8,112,512]{2,1,0:T(8,128)S(1)}, f32[8,112,512]{2,1,0:T(8,128)}, u32[]{:S(2)}) copy-start(f32[8,112,512]{2,1,0:T(8,128)} %get-tuple-element.31) | copy-start | bytes 5505028

commit v2 on v1

--- a/solution.py
+++ b/solution.py
@@ -17,9 +17,19 @@
 HALF = OUTER // 2 + 1
 
 
-def halo_kernel(rows_ref, cols_ref, rows_out, cols_out, circle_ref, lat_send, lat_recv, lon_send, lon_recv, cir_send, cir_recv):
+def wide(tile, width):
+    count = width // INNER
+    return tile if count == 1 else jnp.concatenate([tile] * count, axis=1)
+
+
+def step_kernel(
+    c_ref, ends_ref, state_ref, geo_ref, ccol_ref, clane_ref, meet_ref, inc_ref,
+    rows, cols, rows_in, cols_in, circle, eff, edge, side_cols, pad_p, pad_t, pad_f,
+    lat_send, lat_recv, lon_send, lon_recv, cir_send, cir_recv,
+):
     a, j = lax.axis_index("lat"), lax.axis_index("lon")
     na, nj = lax.axis_size("lat"), lax.axis_size("lon")
+    levels, height, width = state_ref.shape[1:]
     barrier = pltpu.get_barrier_semaphore()
 
     def greet(t, carry):
@@ -27,9 +37,32 @@
         return carry
 
     lax.fori_loop(1, nj, greet, 0)
-
     for near in (lax.rem(a + 1, na), lax.rem(a + na - 1, na)):
         pl.semaphore_signal(barrier, inc=1, device_id=(near, j), device_id_type=MESH)
+
+    order = (0, 0, 1, 2, 3)
+    for s in range(2):
+        for k, f in enumerate(order):
+            inner = 1 if k == 1 else 0
+            r = inner if s == 0 else height - 1 - inner
+            for l in range(levels):
+                rows[s, 8 * k + l : 8 * k + l + 1, :] = state_ref[f, l, r : r + 1, :]
+        rows[s, 40:48, :] = meet_ref[...]
+    lane = lax.broadcasted_iota(jnp.int32, (height, INNER), 1)
+    for s in range(2):
+        packed = jnp.zeros((height, INNER), jnp.float32)
+        for k, f in enumerate(order):
+            inner = 1 if k == 1 else 0
+            source = inner if s == 0 else INNER - 1 - inner
+            start = 0 if s == 0 else width - INNER
+            for l in range(levels):
+                tile = state_ref[f, l, :, start : start + INNER]
+                spot = 8 * k + l
+                shift = (spot - source) % INNER
+                if shift:
+                    tile = pltpu.roll(tile, shift, 1)
+                packed = jnp.where(lane == spot, tile, packed)
+        cols[s] = packed
     pl.semaphore_wait(barrier, nj + 1)
 
     pole = jnp.logical_or(a == 0, a == na - 1)
@@ -38,49 +71,46 @@
     def lat_copy(s):
         target = a - 1 if s == 0 else a + 1
         return pltpu.make_async_remote_copy(
-            rows_ref.at[s], rows_out.at[1 - s], lat_send.at[s], lat_recv.at[1 - s],
+            rows.at[s], rows_in.at[1 - s], lat_send.at[s], lat_recv.at[1 - s],
             device_id=(target, j), device_id_type=MESH)
 
     def lon_copy(s):
         target = lax.rem(j + (nj - 1 if s == 0 else 1), nj)
         return pltpu.make_async_remote_copy(
-            cols_ref.at[s], cols_out.at[1 - s], lon_send.at[s], lon_recv.at[1 - s],
+            cols.at[s], cols_in.at[1 - s], lon_send.at[s], lon_recv.at[1 - s],
             device_id=(a, target), device_id_type=MESH)
 
     def circle_copy(t):
         return pltpu.make_async_remote_copy(
-            rows_ref.at[side], circle_ref.at[j], cir_send.at[t], cir_recv.at[j],
+            rows.at[side], circle.at[j], cir_send.at[t], cir_recv.at[j],
             device_id=(a, lax.rem(j + t, nj)), device_id_type=MESH)
 
     def circle_wait(t):
         source = lax.rem(j + t, nj)
         return pltpu.make_async_remote_copy(
-            rows_ref.at[side], circle_ref.at[source], cir_send.at[t], cir_recv.at[source],
+            rows.at[side], circle.at[source], cir_send.at[t], cir_recv.at[source],
             device_id=(a, source), device_id_type=MESH)
 
-    own = pltpu.make_async_copy(rows_ref.at[side], circle_ref.at[j], cir_recv.at[j])
+    own = pltpu.make_async_copy(rows.at[side], circle.at[j], cir_recv.at[j])
 
     @pl.when(pole)
     def _():
         lax.fori_loop(1, nj, lambda t, c: (circle_copy(t).start(), c)[1], 0)
         own.start()
 
+    @pl.when(a > 0)
+    def _():
+        lat_copy(0).start()
+
+    @pl.when(a < na - 1)
+    def _():
+        lat_copy(1).start()
+
     lon_copy(0).start()
     lon_copy(1).start()
 
     @pl.when(a > 0)
     def _():
-        lat_copy(0).start()
-
-    @pl.when(a < na - 1)
-    def _():
-        lat_copy(1).start()
-
-    lon_copy(0).wait()
-    lon_copy(1).wait()
-
-    @pl.when(a > 0)
-    def _():
         lat_copy(0).wait_send()
         lat_copy(1).wait_recv()
 
@@ -88,6 +118,17 @@
     def _():
         lat_copy(1).wait_send()
         lat_copy(0).wait_recv()
+
+    ccol = wide(ccol_ref[...], width)
+
+    for s in range(2):
+        near, far, u, v, th = (rows_in[s, 8 * k : 8 * k + 8, :] for k in range(5))
+        first = rows[s, 0:8, :]
+        rise = first - far if s == 0 else far - first
+        flux = (v + (-ccol * rise * 0.5 - coriolis * ends_ref[2 * s + 1] * u)) * ends_ref[2 * s]
+        eff[s, 0:8, :] = near
+        eff[s, 8:16, :] = th
+        eff[s, 16:24, :] = flux
 
     @pl.when(pole)
     def _():
@@ -98,25 +139,123 @@
 
         lax.fori_loop(1, nj, finish, 0)
         own.wait()
-
-
-def exchange_halos(rows, cols):
+        column = lax.broadcasted_iota(jnp.int32, (width, width), 0)
+
+        def gather(count, where):
+            def add(s, total):
+                x = circle[s, 0:count, :]
+                high = x.astype(jnp.bfloat16).astype(jnp.float32)
+                rest = x - high
+                middle = rest.astype(jnp.bfloat16).astype(jnp.float32)
+                pieces = jnp.concatenate([high, middle, rest - middle], axis=0).astype(jnp.bfloat16)
+                hit = (column + s * width).astype(jnp.float32) == where
+                chosen = jnp.where(hit, 1.0, 0.0).astype(jnp.bfloat16)
+                return total + jnp.dot(pieces, chosen, preferred_element_type=jnp.float32)
+
+            total = lax.fori_loop(0, nj, add, jnp.zeros((3 * count, width), jnp.float32))
+            return (total[:count] + total[count : 2 * count]) + total[2 * count :]
+
+        met = gather(48, meet_ref[0:1, :])
+        twice = gather(8, met[40:41])
+        near, inner, u, v, th = (met[8 * k : 8 * k + 8] for k in range(5))
+        rise = jnp.where(a == 0, 1.0, -1.0) * (inner - twice)
+        flux = -(v + (-ccol * rise * 0.5 - coriolis * ends_ref[5] * u)) * ends_ref[4]
+        eff[side, 0:8, :] = near
+        eff[side, 8:16, :] = th
+        eff[side, 16:24, :] = flux
+
+    lon_copy(0).wait()
+    lon_copy(1).wait()
+
+    for s in range(2):
+        got = cols_in[s]
+        first = cols[s]
+        far, u, v = (pltpu.roll(got, INNER - 8 * k, 1) for k in (1, 2, 3))
+        rise = first - far if s == 0 else far - first
+        fresh = u + (-clane_ref[0:1, :] * geo_ref[2] * rise * 0.5 + coriolis * geo_ref[1] * v)
+        edge[s] = jnp.where(lane < 40, got, pltpu.roll(fresh, 40, 1))
+
+    lanes = lax.broadcasted_iota(jnp.int32, (8, width), 1)
+
+    def level(l, carry):
+        c = c_ref[l]
+        for k, lane0 in enumerate((0, 32, 40)):
+            side_cols[2 * k] = pltpu.roll(edge[0], INNER - lane0 - l, 1)
+            side_cols[2 * k + 1] = pltpu.roll(edge[1], INNER - 1 - lane0 - l, 1)
+        inside = slice(8, 8 + height)
+        pad_p[inside, :] = state_ref[0, l]
+        pad_t[inside, :] = state_ref[3, l]
+        for k, pad in enumerate((pad_p, pad_t, pad_f)):
+            pad[7:8, :] = eff[0, pl.ds(8 * k + l, 1), :]
+            pad[8 + height : 9 + height, :] = eff[1, pl.ds(8 * k + l, 1), :]
+
+        def zonal(x, k, r):
+            west = jnp.where(lanes == 0, wide(side_cols[2 * k, r, :], width), pltpu.roll(x, 1, 1))
+            east = jnp.where(
+                lanes == width - 1, wide(side_cols[2 * k + 1, r, :], width), pltpu.roll(x, width - 1, 1)
+            )
+            return east - west
+
+        def merid(pad, i):
+            return pad[9 + 8 * i : 17 + 8 * i, :] - pad[7 + 8 * i : 15 + 8 * i, :]
+
+        for i in range(height // 8):
+            r = slice(8 * i, 8 * i + 8)
+            cos, sin, metric = (wide(geo_ref[k, r, :], width) for k in range(3))
+            u, v = state_ref[1, l, r, :], state_ref[2, l, r, :]
+            tend_u = -c * metric * zonal(state_ref[0, l, r, :], 0, r) * 0.5 + coriolis * sin * v
+            tend_v = -c * merid(pad_p, i) * 0.5 - coriolis * sin * u
+            u_new, v_new = u + tend_u, v + tend_v
+            pad_f[8 + 8 * i : 16 + 8 * i, :] = v_new * cos
+            inc_ref[levels + l, r, :] = tend_u
+            inc_ref[2 * levels + l, r, :] = tend_v
+            inc_ref[3 * levels + l, r, :] = (
+                -c * metric * u_new * zonal(state_ref[3, l, r, :], 1, r) * 0.5 - c * v_new * merid(pad_t, i) * 0.5
+            )
+            inc_ref[l, r, :] = zonal(u_new, 2, r) * 0.5
+        for i in range(height // 8):
+            r = slice(8 * i, 8 * i + 8)
+            metric = wide(geo_ref[2, r, :], width)
+            inc_ref[l, r, :] = -(c * metric * (inc_ref[l, r, :] + merid(pad_f, i) * 0.5))
+        return carry
+
+    lax.fori_loop(0, levels, level, 0)
+
+
+def increments_of(state, level_courant, partner, geo, ends):
+    fields, levels, height, width = state.shape
     nj = lax.axis_size("lon")
     vmem = pl.BlockSpec(memory_space=pltpu.VMEM)
+    smem = pl.BlockSpec(memory_space=pltpu.SMEM)
     dma = pltpu.SemaphoreType.DMA
+    f32 = jnp.float32
+    ccol = jnp.broadcast_to(level_courant[:, None], (levels, INNER))
+    clane = jnp.broadcast_to(jnp.pad(level_courant, (0, INNER - levels))[None], (8, INNER))
+    meet = jnp.broadcast_to(partner.astype(f32)[None], (8, width))
     return pl.pallas_call(
-        halo_kernel,
-        out_shape=(
-            jax.ShapeDtypeStruct(rows.shape, jnp.float32),
-            jax.ShapeDtypeStruct(cols.shape, jnp.float32),
-            jax.ShapeDtypeStruct((nj,) + rows.shape[1:], jnp.float32),
+        step_kernel,
+        out_shape=jax.ShapeDtypeStruct((fields * levels, height, width), f32),
+        in_specs=[smem, smem, vmem, vmem, vmem, vmem, vmem],
+        out_specs=vmem,
+        scratch_shapes=[
+            pltpu.VMEM((2, 48, width), f32),
+            pltpu.VMEM((2, height, INNER), f32),
+            pltpu.VMEM((2, 48, width), f32),
+            pltpu.VMEM((2, height, INNER), f32),
+            pltpu.VMEM((nj, 48, width), f32),
+            pltpu.VMEM((2, 24, width), f32),
+            pltpu.VMEM((2, height, INNER), f32),
+            pltpu.VMEM((6, height, INNER), f32),
+            pltpu.VMEM((height + 16, width), f32),
+            pltpu.VMEM((height + 16, width), f32),
+            pltpu.VMEM((height + 16, width), f32),
+            dma((2,)), dma((2,)), dma((2,)), dma((2,)), dma((nj,)), dma((nj,)),
+        ],
+        compiler_params=pltpu.CompilerParams(
+            collective_id=0, has_side_effects=True, vmem_limit_bytes=40 * 1024 * 1024
         ),
-        in_specs=[vmem, vmem],
-        out_specs=(vmem, vmem, vmem),
-        scratch_shapes=[dma((2,)), dma((2,)), dma((2,)), dma((2,)), dma((nj,)), dma((nj,))],
-        compiler_params=pltpu.CompilerParams(collective_id=0, has_side_effects=True),
-        name="halos",
-    )(rows, cols)
+        name="step",
+    )(level_courant, ends, state, geo, ccol, clane, meet)
 
 
 def real_forward(values):
@@ -401,74 +540,15 @@
 
     first_row = a * rows_n
     cos1, sin1 = geometry(first_row + jnp.arange(rows_n, dtype=jnp.int32))
-    cos_lat, sin_lat = cos1[:, None], sin1[:, None]
     metric1 = 1.0 / jnp.maximum(cos1, cos_floor)
-    metric = metric1[:, None]
-    c1 = level_courant[:, None]
-    courant = level_courant[:, None, None]
-    p, u, v, th = state[0], state[1], state[2], state[3]
-    meet = jnp.broadcast_to(partner.astype(jnp.float32)[None, :], (8, cols_n))
-
-    def row_pack(outer, inner):
-        return jnp.concatenate(
-            [p[:, outer], p[:, inner], u[:, outer], v[:, outer], th[:, outer], meet], axis=0
-        )
-
-    def col_pack(outer, inner):
-        return jnp.concatenate(
-            [p[:, :, outer], p[:, :, inner], u[:, :, outer], v[:, :, outer], th[:, :, outer]], axis=0
-        )
-
-    rows = jnp.stack([row_pack(0, 1), row_pack(rows_n - 1, rows_n - 2)])
-    cols = jnp.stack([col_pack(0, 1), col_pack(cols_n - 1, cols_n - 2)])
-    rows_in, cols_in, circle = exchange_halos(rows, cols)
-
-    def fields_of(pack):
-        return [pack[8 * k : 8 * k + 8] for k in range(5)]
-
-    at_south, at_north = a == 0, a == na - 1
-    whole = jnp.transpose(circle, (1, 0, 2)).reshape(circle.shape[1], -1)
-    met = jnp.take(whole, partner, axis=1)
-    twice = jnp.clip(met[40].astype(jnp.int32), 0, whole.shape[1] - 1)
-    p_twice = jnp.take(whole[:8], twice, axis=1)
-    p_met, p_met_in, u_met, v_met, th_met = fields_of(met)
-    cos_end = jnp.where(at_south, cos1[0], cos1[-1])
-    sin_end = jnp.where(at_south, sin1[0], sin1[-1])
-    rise = jnp.where(at_south, p_met_in - p_twice, p_twice - p_met_in)
-    flux_met = -(v_met + (-c1 * rise * 0.5 - coriolis * sin_end * u_met)) * cos_end
-
-    ps, ps2, us, vs, ths = fields_of(rows_in[0])
-    pn, pn2, un, vn, thn = fields_of(rows_in[1])
+    geo = jnp.broadcast_to(jnp.stack([cos1, sin1, metric1])[:, :, None], (3, rows_n, INNER))
     cos_s, sin_s = geometry(first_row - 1)
     cos_n, sin_n = geometry(first_row + rows_n)
-    flux_s = (vs + (-c1 * (p[:, 0] - ps2) * 0.5 - coriolis * sin_s * us)) * cos_s
-    flux_n = (vn + (-c1 * (pn2 - p[:, -1]) * 0.5 - coriolis * sin_n * un)) * cos_n
-    ps, ths, flux_s = (jnp.where(at_south, m, o) for m, o in ((p_met, ps), (th_met, ths), (flux_met, flux_s)))
-    pn, thn, flux_n = (jnp.where(at_north, m, o) for m, o in ((p_met, pn), (th_met, thn), (flux_met, flux_n)))
-
-    pw, pw2, uw, vw, thw = fields_of(cols_in[0])
-    pe, pe2, ue, ve, the = fields_of(cols_in[1])
-    u_west = uw + (-c1 * metric1 * (p[:, :, 0] - pw2) * 0.5 + coriolis * sin1 * vw)
-    u_east = ue + (-c1 * metric1 * (pe2 - p[:, :, -1]) * 0.5 + coriolis * sin1 * ve)
-
-    def zonal(f, west, east):
-        return jnp.concatenate([f[:, :, 1:], east[:, :, None]], axis=2) - jnp.concatenate(
-            [west[:, :, None], f[:, :, :-1]], axis=2
-        )
-
-    def merid(f, south, north):
-        return jnp.concatenate([f[:, 1:], north[:, None, :]], axis=1) - jnp.concatenate(
-            [south[:, None, :], f[:, :-1]], axis=1
-        )
-
-    tend_u = -courant * metric * zonal(p, pw, pe) * 0.5 + coriolis * sin_lat * v
-    tend_v = -courant * merid(p, ps, pn) * 0.5 - coriolis * sin_lat * u
-    u_new = u + tend_u
-    v_new = v + tend_v
-    flux = v_new * cos_lat
-    divergence = courant * metric * (zonal(u_new, u_west, u_east) * 0.5 + merid(flux, flux_s, flux_n) * 0.5)
-    tend_t = -courant * metric * u_new * zonal(th, thw, the) * 0.5 - courant * v_new * merid(th, ths, thn) * 0.5
-    inc = jnp.concatenate([-divergence, tend_u, tend_v, tend_t])
+    south = a == 0
+    ends = jnp.stack([
+        cos_s, sin_s, cos_n, sin_n, jnp.where(south, cos1[0], cos1[-1]), jnp.where(south, sin1[0], sin1[-1])
+    ])
+    inc = increments_of(state, level_courant, partner, geo, ends)
 
     quarter = na // 4
     pairs = [(i, 2 * quarter - 1 - i if i < na // 2 else 2 * na - 2 * quarter - 1 - i) for i in range(na)]

time: 276 us -> 235 us (0.85)
  local copies, waits for them, and re-layouts: 57.3 us -> 17.6 us
  other arithmetic: 31.3 us -> 15.3 us
  Pallas kernels: 183 us -> 198 us
    slice x27 -> x2, local copies, waits for them, and re-layouts: 29.5 us -> 1.25 us  [the longest x1 0.64 us: per_device(): sin1[-1]]
    pallas_call x1, Pallas kernels: 16.7 us -> 31.7 us  [increments_of(): pl.pallas_call(step_kernel, out_shape=jax.ShapeDtypeStruct((fields * leve...]
    sub x3 -> x0, other arithmetic: 11.4 us -> none  [the longest x1 7.39 us: per_device(): -courant * metric * u_new * zonal(th, thw, the) * 0.5]
    squeeze x2 -> x0, local copies, waits for them, and re-layouts: 7.87 us -> none  [per_device(): p, u, v, th = (state[0], state[1], state[2], state[3])]
    unnamed x75 -> x16, local copies, waits for them, and re-layouts: 5.45 us -> 13 us
    gather x4 -> x0, local copies, waits for them, and re-layouts: 7 us -> none  [the longest x2 4.27 us: per_device(): p_twice = jnp.take(whole[:8], twice, axis=1)]
    add x1, other arithmetic: 7.06 us -> 13.8 us  [per_device(): result = state.reshape(inc.shape) + jnp.where(chosen, smooth, inc)]
    neg x2 -> x0, other arithmetic: 4.33 us -> none  [the longest x1 4.32 us: per_device(): inc = jnp.concatenate([-divergence, tend_u, tend_v, tend_t])]
  transfers between devices with their start and end apart: 1 -> 1, of which waited for: 0 -> 0; matrix products, arithmetic and copies ran while one was open for 28% -> 5% of each run, Pallas kernels for 6% -> 14%
where the time goes in v2:
time: 235 us
  Pallas kernels  198 us (84%)
  local copies, waits for them, and re-layouts  17.6 us (7%)
  other arithmetic  15.3 us (7%)
  between operations  2.98 us (1%)
    pallas_call x1, Pallas kernels, filter_circles(): pl.pallas_call(functools.partial(circle_kernel, upd, parts), out_shape=ja...  167 us
    pallas_call x1, Pallas kernels, increments_of(): pl.pallas_call(step_kernel, out_shape=jax.ShapeDtypeStruct((fields * leve...  31.7 us
    add x1, other arithmetic, per_device(): result = state.reshape(inc.shape) + jnp.where(chosen, smooth, inc)  13.8 us
    unnamed x16, local copies, waits for them, and re-layouts  13 us
  transfers between devices with their start and end apart: 1, of which 0 were waited for; matrix products, arithmetic and copies ran while one was open for 5% of the time, Pallas kernels for 14%

profile of v2, /device:TPU:10, one launch (start us, length us, event | category | flops | bytes accessed | tf_op | source)
XLA Modules:
  0.0 234.8 jit_solution(11944171013223843656)
XLA Ops:
  0.0 0.0 collective-permute-start
  0.5 0.6 fusion.11
  1.1 0.6 fusion.12
  1.7 0.7 convert_element_type.36
  2.4 6.2 %reverse = f32[16,2048]{1,0:T(8,128)S(1)} reverse(f32[16,2048]{1,0:T(8,128)} %param.11), dimensions={1} | reverse | bytes 262144
  8.6 0.1 slice.29
  8.8 1.1 concatenate.3
  9.8 0.3 reshape.58
  10.2 0.3 copy.11
  10.5 0.7 compare_and_fusion
  11.2 0.7 pad.4
  14.4 0.1 stack.33.ends_ref
  14.4 0.7 broadcast_in_dim.15.ccol_ref
  15.2 0.1 broadcast_in_dim.14.geo_ref
  15.3 0.0 copy-start.5
  15.3 0.7 copy-done.5
  15.9 0.0 copy-start.6
  15.9 0.0 copy-start.2
  15.9 0.0 copy-start.3
  16.0 0.0 copy-start.4
  16.0 31.7 %step.1.inc_ref = f32[32,112,512]{2,1,0:T(8,128)S(1)} custom-call(f32[8]{0:T(128)S(1)} %copy-done.5, f32[6]{0:T(128)S(1)} %stack.33.ends_ref, f32[4,8,112,512]{3,2,1,0:T(8,128)} %state_ref.1, f32[3,112,128]{2,1,0:T(8,128)S(1)} %broadcast_in_dim.14.geo_ref, f32[8,128]{1,0:T(8,128)S(1)} %broadcast_in_dim.15.ccol_ref, f32[8,128]{1,0:T(8,128)S(1)} %broadcast_in_dim.16.clane_ref, ...), custom_call_target="tpu_custom_call" | custom-call | tf_op jit(solution)/shard_map/step/pallas_call | solution.py:235
  47.7 0.0 copy-start
  47.7 3.0 %copy-done = f32[32,112,512]{2,1,0:T(8,128)} copy-done((f32[32,112,512]{2,1,0:T(8,128)}, f32[32,112,512]{2,1,0:T(8,128)S(1)}, u32[]{:S(2)}) %copy-start) | copy-done | bytes 7340056
  50.7 0.0 collective-permute-done
  50.7 0.0 copy-done.6
  50.7 0.1 eq.28
  50.8 0.6 convolution_bitcast_fusion.damp_ref
  51.4 0.0 copy-done.2
  51.4 0.0 copy-done.3
  51.4 0.0 copy-done.4
  51.5 166.6 %circles.1 = f32[32,112,512]{2,1,0:T(8,128)S(1)} custom-call(f32[32,112,512]{2,1,0:T(8,128)} %copy-done, f32[2,17,56,128]{3,2,1,0:T(8,128)S(1)} %convolution_bitcast_fusion.damp_ref, f32[2,17,128]{2,1,0:T(8,128)S(1)} %copy-done.4, bf16[2,256,256]{2,1,0:T(8,128)(2,1)S(1)} %copy-done.3, bf16[2,256,256]{2,1,0:T(8,128)(2,1)S(1)} %copy-done.2), custom_call_target="tpu_custom_call" | custom-call | tf_op jit(solution)/shard_map/circles/pallas_call | solution.py:510
  218.1 0.0 copy-start.1
  218.1 2.9 %copy-done.1 = f32[32,112,512]{2,1,0:T(8,128)} copy-done((f32[32,112,512]{2,1,0:T(8,128)}, f32[32,112,512]{2,1,0:T(8,128)S(1)}, u32[]{:S(2)}) %copy-start.1) | copy-done | bytes 7340056
  221.0 13.8 %bitcast_add_fusion = f32[32,112,512]{2,1,0:T(8,128)} fusion(f32[4,8,112,512]{3,2,1,0:T(8,128)} %state_ref.1, f32[32,112,512]{2,1,0:T(8,128)} %copy-done.1, f32[32,112,512]{2,1,0:T(8,128)} %copy-done, pred[112]{0:T(512)(128)(4,1)S(1)} %compare_and_fusion), kind=kLoop, calls=%fused_computation | loop fusion | flops 3670016 | bytes 29360240 | tf_op jit(solution)/shard_map/add | solution.py:570
  (8 shorter events, 0.2 us)
Async XLA Ops:
  0.0 50.7 %collective-permute-start = (s32[112]{0:T(128)}, s32[112]{0:T(128)S(1)}, u32[]{:S(2)}, u32[]{:S(2)}) collective-permute-start(s32[112]{0:T(128)} %param.13), channel_id=1, source_target_pairs={{0,8},{8,0},{16,24},{24,16},{1,9},{9,1},{17,25},{25,17},{2,10},{10... | collective-permute-start | bytes 1352 | tf_op jit(solution)/shard_map/ppermute | solution.py:556
  15.3 0.7 copy-start.5
  15.9 34.8 %copy-start.6 = (s32[112]{0:T(128)S(1)}, s32[112]{0:T(128)}, u32[]{:S(2)}) copy-start(s32[112]{0:T(128)} %param.13) | copy-start | bytes 1348
  15.9 35.5 %copy-start.2 = (bf16[2,256,256]{2,1,0:T(8,128)(2,1)S(1)}, bf16[2,256,256]{2,1,0:T(8,128)(2,1)}, u32[]{:S(2)}) copy-start(bf16[2,256,256]{2,1,0:T(8,128)(2,1)} %constant.53.clone.bwd_ref) | copy-start | bytes 786436
  15.9 35.5 %copy-start.3 = (bf16[2,256,256]{2,1,0:T(8,128)(2,1)S(1)}, bf16[2,256,256]{2,1,0:T(8,128)(2,1)}, u32[]{:S(2)}) copy-start(bf16[2,256,256]{2,1,0:T(8,128)(2,1)} %constant.52.clone.fwd_ref) | copy-start | bytes 786436
  16.0 35.5 %copy-start.4 = (f32[2,17,128]{2,1,0:T(8,128)S(1)}, f32[2,17,128]{2,1,0:T(8,128)}, u32[]{:S(2)}) copy-start(f32[2,17,128]{2,1,0:T(8,128)} %constant.51.clone.twid_ref) | copy-start | bytes 52228
  47.7 3.1 %copy-start = (f32[32,112,512]{2,1,0:T(8,128)}, f32[32,112,512]{2,1,0:T(8,128)S(1)}, u32[]{:S(2)}) copy-start(f32[32,112,512]{2,1,0:T(8,128)S(1)} %step.1.inc_ref) | copy-start | bytes 22020100
  218.1 2.9 %copy-start.1 = (f32[32,112,512]{2,1,0:T(8,128)}, f32[32,112,512]{2,1,0:T(8,128)S(1)}, u32[]{:S(2)}) copy-start(f32[32,112,512]{2,1,0:T(8,128)S(1)} %circles.1) | copy-start | bytes 22020100

commit v3 on v2

--- a/solution.py
+++ b/solution.py
@@ -23,8 +23,8 @@
 
 
 def step_kernel(
-    c_ref, ends_ref, state_ref, geo_ref, ccol_ref, clane_ref, meet_ref, inc_ref,
-    rows, cols, rows_in, cols_in, circle, eff, edge, side_cols, pad_p, pad_t, pad_f,
+    c_ref, ends_ref, state_ref, geo_ref, ccol_ref, clane_ref, meet_ref, out_ref,
+    inc_ref, out_sem, rows, cols, rows_in, cols_in, circle, eff, edge, side_cols, pad_p, pad_t, pad_f,
     lat_send, lat_recv, lon_send, lon_recv, cir_send, cir_recv,
 ):
     a, j = lax.axis_index("lat"), lax.axis_index("lon")
@@ -177,6 +177,10 @@
 
     lanes = lax.broadcasted_iota(jnp.int32, (8, width), 1)
 
+    def leave(f, l):
+        spot = f * levels + l
+        return pltpu.make_async_copy(inc_ref.at[spot], out_ref.at[spot], out_sem.at[spot])
+
     def level(l, carry):
         c = c_ref[l]
         for k, lane0 in enumerate((0, 32, 40)):
@@ -217,9 +221,18 @@
             r = slice(8 * i, 8 * i + 8)
             metric = wide(geo_ref[2, r, :], width)
             inc_ref[l, r, :] = -(c * metric * (inc_ref[l, r, :] + merid(pad_f, i) * 0.5))
+        for f in range(4):
+            leave(f, l).start()
         return carry
 
     lax.fori_loop(0, levels, level, 0)
+
+    def settle(l, carry):
+        for f in range(4):
+            leave(f, l).wait()
+        return carry
+
+    lax.fori_loop(0, levels, settle, 0)
 
 
 def increments_of(state, level_courant, partner, geo, ends):
@@ -236,8 +249,10 @@
         step_kernel,
         out_shape=jax.ShapeDtypeStruct((fields * levels, height, width), f32),
         in_specs=[smem, smem, vmem, vmem, vmem, vmem, vmem],
-        out_specs=vmem,
+        out_specs=pl.BlockSpec(memory_space=pl.ANY),
         scratch_shapes=[
+            pltpu.VMEM((fields * levels, height, width), f32),
+            dma((fields * levels,)),
             pltpu.VMEM((2, 48, width), f32),
             pltpu.VMEM((2, height, INNER), f32),
             pltpu.VMEM((2, 48, width), f32),
@@ -252,7 +267,7 @@
             dma((2,)), dma((2,)), dma((2,)), dma((2,)), dma((nj,)), dma((nj,)),
         ],
         compiler_params=pltpu.CompilerParams(
-            collective_id=0, has_side_effects=True, vmem_limit_bytes=40 * 1024 * 1024
+            collective_id=0, has_side_effects=True, vmem_limit_bytes=58 * 1024 * 1024
         ),
         name="step",
     )(level_courant, ends, state, geo, ccol, clane, meet)
@@ -522,7 +537,7 @@
             dma((upd, 2 * nj)),
         ],
         compiler_params=pltpu.CompilerParams(
-            collective_id=1, has_side_effects=True, vmem_limit_bytes=40 * 1024 * 1024
+            collective_id=1, has_side_effects=True, vmem_limit_bytes=58 * 1024 * 1024
         ),
         name="circles",
     )(inc, weights, twiddle, forward, backward)
@@ -557,10 +572,15 @@
     parts = 2
     count = damp_table.shape[0]
     length = OUTER * INNER
-    full = jnp.concatenate(
-        [jnp.ones((count, 1), jnp.float32), damp_table, jnp.flip(damp_table[:, :-1], axis=1)], axis=1
-    )
-    grid = jnp.transpose(full.reshape(count, INNER, OUTER), (0, 2, 1))[:, :HALF] * (1.0 / length)
+    half = INNER // 2
+    exact = lax.Precision.HIGHEST
+    lower = jnp.concatenate([jnp.ones((count, 1), jnp.float32), damp_table[:, :-1]], axis=1)
+    lower = jnp.transpose(lower.reshape(count, half, OUTER)[:, :, :HALF], (0, 2, 1))
+    turned = damp_table.reshape(count, half, OUTER)[:, :, OUTER - HALF :]
+    turn_m = jnp.asarray(np.eye(half, dtype=np.float32)[::-1].copy())
+    turn_k = jnp.asarray(np.eye(HALF, dtype=np.float32)[::-1].copy())
+    upper = jnp.einsum("tmj,jk,mn->tkn", turned, turn_k, turn_m, precision=exact)
+    grid = jnp.concatenate([lower, upper], axis=2) * (1.0 / length)
     pick = (table[:, None] == jnp.arange(count, dtype=jnp.int32)[None, :]).astype(jnp.float32)
     weights = jnp.einsum(
         "hrt,tkm->hkrm", pick.reshape(parts, rows_n // parts, count), grid, precision=lax.Precision.HIGHEST

time: 235 us -> 233 us (level)
  local copies, waits for them, and re-layouts: 17.6 us -> 8.35 us
  matrix products: 0.59 us -> 4.76 us
  Pallas kernels: 198 us -> 201 us
    unnamed x16 -> x3, local copies, waits for them, and re-layouts: 13 us -> 0.23 us
    dot_general x0 -> x2, matrix products: none -> 3.18 us  [per_device(): jnp.einsum('tmj,jk,mn->tkn', turned, turn_k, turn_m, precision=exact)]
  transfers between devices with their start and end apart: 1 -> 1, of which waited for: 0 -> 0; matrix products, arithmetic and copies ran while one was open for 5% -> 6% of each run, Pallas kernels for 14% -> 14%
where the time goes in v3:
time: 233 us; the launch traced here: 232 us
  Pallas kernels  201 us (86%)
  other arithmetic  15.3 us (7%)
  local copies, waits for them, and re-layouts  8.35 us (4%)
  matrix products  4.76 us (2%)
  between operations  2.95 us (1%)
    pallas_call x1, Pallas kernels, filter_circles(): pl.pallas_call(functools.partial(circle_kernel, upd, parts), out_shape=ja...  168 us
    pallas_call x1, Pallas kernels, increments_of(): pl.pallas_call(step_kernel, out_shape=jax.ShapeDtypeStruct((fields * leve...  32.9 us
    add x1, other arithmetic, per_device(): result = state.reshape(inc.shape) + jnp.where(chosen, smooth, inc)  13.8 us
  transfers between devices with their start and end apart: 1, of which 0 were waited for; matrix products, arithmetic and copies ran while one was open for 6% of the time, Pallas kernels for 14%

profile of v3, /device:TPU:10, one launch (start us, length us, event | category | flops | bytes accessed | tf_op | source)
XLA Modules:
  0.0 232.1 jit_solution(15780002346603633806)
XLA Ops:
  0.0 0.0 collective-permute-start
  0.5 0.6 fusion.17
  1.1 0.6 fusion.18
  1.7 0.7 convert_element_type.36
  2.4 1.1 reshape.62
  3.5 1.0 concatenate.6
  4.5 0.2 reshape.61
  4.7 0.2 copy.18
  4.9 0.7 compare_and_fusion
  5.6 0.7 pad.5
  8.7 2.2 fusion
  10.9 1.0 convolution_bitcast_fusion.1
  12.0 0.6 stack.33.ends_ref
  12.6 0.6 broadcast_in_dim.16.clane_ref
  13.2 1.3 broadcast_in_dim.15.ccol_ref
  14.5 0.6 broadcast_in_dim.17.meet_ref
  15.1 0.8 broadcast_in_dim.14.geo_ref
  15.8 0.0 copy-start
  15.9 32.9 %step.1.inc_ref = f32[32,112,512]{2,1,0:T(8,128)} custom-call(f32[8]{0:T(128)} %c_ref.1, f32[6]{0:T(128)} %stack.33.ends_ref, f32[4,8,112,512]{3,2,1,0:T(8,128)} %state_ref.1, f32[3,112,128]{2,1,0:T(8,128)} %broadcast_in_dim.14.geo_ref, f32[8,128]{1,0:T(8,128)} %broadcast_in_dim.15.ccol_ref, f32[8,128]{1,0:T(8,128)} %broadcast_in_dim.16.clane_ref, ...), custom_call_target="tpu_custom_call" | custom-call | tf_op jit(solution)/shard_map/step/pallas_call | solution.py:248
  48.8 0.0 collective-permute-done
  48.8 0.0 copy-done
  48.8 0.1 eq.28
  48.9 1.6 convolution_bitcast_fusion.damp_ref
  50.5 167.8 %circles.1 = f32[32,112,512]{2,1,0:T(8,128)} custom-call(f32[32,112,512]{2,1,0:T(8,128)} %step.1.inc_ref, f32[2,17,56,128]{3,2,1,0:T(8,128)} %convolution_bitcast_fusion.damp_ref, f32[2,17,128]{2,1,0:T(8,128)} %constant.57.clone.twid_ref, bf16[2,256,256]{2,1,0:T(8,128)(2,1)} %constant.58.clone.fwd_ref, bf16[2,256,256]{2,1,0:T(8,128)(2,1)} %constant.59.clone.bwd_ref), custom_call_target="tpu_custom_call" | custom-call | tf_op jit(solution)/shard_map/circles/pallas_call | solution.py:525
  218.4 13.8 %bitcast_add_fusion = f32[32,112,512]{2,1,0:T(8,128)} fusion(f32[4,8,112,512]{3,2,1,0:T(8,128)} %state_ref.1, f32[32,112,512]{2,1,0:T(8,128)} %circles.1, f32[32,112,512]{2,1,0:T(8,128)} %step.1.inc_ref, pred[112]{0:T(512)(128)(4,1)S(1)} %compare_and_fusion), kind=kLoop, calls=%fused_computation | loop fusion | flops 3670016 | bytes 29360240 | tf_op jit(solution)/shard_map/add | solution.py:590
  (5 shorter events, 0.2 us)
Async XLA Ops:
  0.0 48.8 %collective-permute-start = (s32[112]{0:T(128)}, s32[112]{0:T(128)S(1)}, u32[]{:S(2)}, u32[]{:S(2)}) collective-permute-start(s32[112]{0:T(128)} %param.15), channel_id=1, source_target_pairs={{0,8},{8,0},{16,24},{24,16},{1,9},{9,1},{17,25},{25,17},{2,10},{10... | collective-permute-start | bytes 1352 | tf_op jit(solution)/shard_map/ppermute | solution.py:571
  15.8 33.0 %copy-start = (s32[112]{0:T(128)S(1)}, s32[112]{0:T(128)}, u32[]{:S(2)}) copy-start(s32[112]{0:T(128)} %param.15) | copy-start | bytes 1348

commit v4 on v3

--- a/solution.py
+++ b/solution.py
@@ -513,7 +513,7 @@
     return jnp.asarray(twiddle), jnp.asarray(pair(forward)), jnp.asarray(pair(forward.T))
 
 
-def filter_circles(inc, weights, parts):
+def filter_circles(inc, weights, parts, ident):
     nj = lax.axis_size("lon")
     stacks, rows, width = inc.shape
     upd = stacks * parts // (2 * nj)
@@ -537,9 +537,9 @@
             dma((upd, 2 * nj)),
         ],
         compiler_params=pltpu.CompilerParams(
-            collective_id=1, has_side_effects=True, vmem_limit_bytes=58 * 1024 * 1024
+            collective_id=ident, has_side_effects=True, vmem_limit_bytes=58 * 1024 * 1024
         ),
-        name="circles",
+        name=f"circles{rows}",
     )(inc, weights, twiddle, forward, backward)
 
 
@@ -568,8 +568,11 @@
     quarter = na // 4
     pairs = [(i, 2 * quarter - 1 - i if i < na // 2 else 2 * na - 2 * quarter - 1 - i) for i in range(na)]
     active = (a < quarter) | (a >= na - quarter)
-    table = jnp.where(active, row_table, lax.ppermute(row_table, "lat", pairs))
-    parts = 2
+    codes = jnp.stack([row_flag, row_table])
+    codes = jnp.where(active, codes, lax.ppermute(codes, "lat", pairs))
+    flagged, table = codes[0] == 1, codes[1]
+    bands = lax.all_gather(row_flag, "lat")
+    fullest = jnp.max(jnp.sum((bands == 1).astype(jnp.int32), axis=1))
     count = damp_table.shape[0]
     length = OUTER * INNER
     half = INNER // 2
@@ -582,10 +585,30 @@
     upper = jnp.einsum("tmj,jk,mn->tkn", turned, turn_k, turn_m, precision=exact)
     grid = jnp.concatenate([lower, upper], axis=2) * (1.0 / length)
     pick = (table[:, None] == jnp.arange(count, dtype=jnp.int32)[None, :]).astype(jnp.float32)
-    weights = jnp.einsum(
-        "hrt,tkm->hkrm", pick.reshape(parts, rows_n // parts, count), grid, precision=lax.Precision.HIGHEST
+    rank = jnp.cumsum(flagged.astype(jnp.int32)) - 1
+    spots = jnp.arange(rows_n, dtype=jnp.int32)
+    packing = ((rank[None, :] == spots[:, None]) & flagged[None, :]).astype(jnp.float32)
+    fewest = max(1, lax.axis_size("lon") * 2 // (fields_n * levels_n))
+    unit = 8 * fewest
+    sizes = [rows_n * 11 // 14 // unit * unit, rows_n * 12 // 14 // unit * unit, rows_n]
+
+    def smoothed(ident, kept, inc):
+        parts = fewest if kept % 16 else 2
+        mover = None if kept == rows_n else packing[:kept]
+        choice = pick if mover is None else jnp.dot(mover, pick, precision=exact)
+        weights = jnp.einsum(
+            "hrt,tkm->hkrm", choice.reshape(parts, kept // parts, count), grid, precision=exact
+        )
+        if mover is None:
+            return filter_circles(inc, weights, parts, ident)
+        packed = jnp.einsum("kr,frw->fkw", mover, inc, precision=exact)
+        packed = filter_circles(packed, weights, parts, ident)
+        return jnp.einsum("kr,fkw->frw", mover, packed, precision=exact)
+
+    branch = sum((fullest > size).astype(jnp.int32) for size in sizes[:-1])
+    smooth = lax.switch(
+        branch, [functools.partial(smoothed, 1 + n, size) for n, size in enumerate(sizes)], inc
     )
-    smooth = filter_circles(inc, weights, parts)
     chosen = (active & (row_flag == 1))[None, :, None]
     result = state.reshape(inc.shape) + jnp.where(chosen, smooth, inc)
     return result.reshape(state.shape)

time: 233 us -> 228 us (0.979)
  Pallas kernels: 201 us -> 165 us
  matrix products: 4.76 us -> 24.5 us
  blocking collectives: 0 us -> 4.93 us
    pallas_call x1, Pallas kernels: 168 us -> 133 us  [filter_circles(): pl.pallas_call(functools.partial(circle_kernel, upd, parts), out_shape=ja...]
    dot_general x1 -> x4, matrix products: 1.58 us -> 21.3 us  [the longest x1 9.99 us: smoothed(): return jnp.einsum('kr,fkw->frw', mover, packed, precision=exact)]
    unnamed x0 -> x1, blocking collectives: none -> 4.93 us
  transfers between devices with their start and end apart: 1 -> 1, of which waited for: 0 -> 0; matrix products, arithmetic and copies ran while one was open for 6% -> 7% of each run, Pallas kernels for 14% -> 14%
where the time goes in v4:
time: 228 us
  Pallas kernels  165 us (72%)
  matrix products  24.5 us (11%)
  other arithmetic  17.1 us (8%)
  local copies, waits for them, and re-layouts  10.6 us (5%)
  between operations  4.97 us (2%)
  blocking collectives  4.93 us (2%)
    pallas_call x1, Pallas kernels, filter_circles(): pl.pallas_call(functools.partial(circle_kernel, upd, parts), out_shape=ja...  133 us
    pallas_call x1, Pallas kernels, increments_of(): pl.pallas_call(step_kernel, out_shape=jax.ShapeDtypeStruct((fields * leve...  32.8 us
    add x1, other arithmetic, per_device(): result = state.reshape(inc.shape) + jnp.where(chosen, smooth, inc)  13.8 us
    dot_general x1, matrix products, smoothed(): return jnp.einsum('kr,fkw->frw', mover, packed, precision=exact)  9.99 us
    dot_general x1, matrix products, smoothed(): packed = jnp.einsum('kr,frw->fkw', mover, inc, precision=exact)  9.41 us
    unnamed x1, blocking collectives  4.93 us
  transfers between devices with their start and end apart: 1, of which 0 were waited for; matrix products, arithmetic and copies ran while one was open for 7% of the time, Pallas kernels for 14%

profile of v4, /device:TPU:10, one launch (start us, length us, event | category | flops | bytes accessed | tf_op | source)
XLA Modules:
  0.0 227.6 jit_solution(3206015077524296136)
XLA Ops:
  0.0 0.7 pad_add_fusion
  0.7 0.0 collective-permute-start
  1.2 0.7 compare_and_fusion
  1.9 0.6 fusion.28
  2.4 0.6 fusion.29
  3.0 0.7 convert_element_type.59
  3.7 1.2 dynamic-slice
  5.6 0.9 dynamic-update-slice
  6.5 4.9 %all-reduce.2 = s32[448]{0:T(512)S(1)} all-reduce(s32[448]{0:T(512)S(1)} %dynamic-update-slice), channel_id=2, replica_groups=mesh['lat'=4,'lon'=8] {'lat'}, use_global_device_ids=true, to_apply=%add.2 | all-reduce | flops 448 | bytes 3584
  11.4 0.1 reshape.101
  11.5 0.1 reduce_sum.9
  11.6 0.6 reduce_max.9
  13.6 1.1 reshape.95
  14.6 1.0 concatenate.6
  15.6 0.2 reshape.94
  15.8 0.2 copy.43
  16.0 0.7 pad.5
  16.7 2.1 fusion.18
  18.8 1.1 convolution_bitcast_fusion.8
  19.9 0.1 maximum_multiply_fusion
  22.5 0.7 stack.42.ends_ref
  23.2 0.6 broadcast_in_dim.16.clane_ref
  23.8 1.3 broadcast_in_dim.15.ccol_ref
  25.1 0.6 broadcast_in_dim.17.meet_ref
  25.7 0.8 broadcast_in_dim.14.geo_ref
  26.5 0.0 copy-start.3
  26.5 0.0 copy-start.4
  26.5 0.0 copy-start
  26.5 0.0 copy-start.1
  26.5 0.0 copy-start.2
  26.5 32.8 %step.1 = f32[32,112,512]{2,1,0:T(8,128)} custom-call(f32[8]{0:T(128)} %c_ref.1, f32[6]{0:T(128)} %stack.42.ends_ref, f32[4,8,112,512]{3,2,1,0:T(8,128)} %state_ref.1, f32[3,112,128]{2,1,0:T(8,128)} %broadcast_in_dim.14.geo_ref, f32[8,128]{1,0:T(8,128)} %broadcast_in_dim.15.ccol_ref, f32[8,128]{1,0:T(8,128)} %broadcast_in_dim.16.clane_ref, ...), custom_call_target="tpu_custom_call" | custom-call | tf_op jit(solution)/shard_map/step/pallas_call | solution.py:248
  59.3 0.0 collective-permute-done
  59.3 0.0 copy-done.3
  59.3 0.0 copy-done.4
  59.4 0.1 copy.31
  59.5 0.2 reduce-window.8
  59.6 0.1 add_reduce_fusion
  59.8 0.0 copy-done
  59.8 0.0 copy-done.1
  59.8 0.0 copy-done.2
  59.8 154.0 %conditional.1 = (f32[32,112,512]{2,1,0:T(8,128)}) conditional(s32[]{:T(128)} %clamp.3, (f32[112,112]{1,0:T(8,128)S(1)}, f32[32,112,512]{2,1,0:T(8,128)}, f32[112,16]{0,1:T(8,128)S(1)}, f32[16,17,128]{2,1,0:T(8,128)S(1)}, f32[2,17,128]{2,1,0:T(8,128)S(1)}, /*index=5*/bf16[2,256,256]{2,1,0:T(8,128)(2,1)S(1)}, ...), branch_computations={%region_3.4_spmd, %region_4.5_spmd, %region_5.6_spmd} | conditional | flops 4270030848 | bytes 28418056 | solution.py:609
  59.8 0.2 convolution_bitcast_fusion.3
  60.0 1.7 convolution_bitcast_fusion.2.damp_ref
  61.7 9.4 %convolution_bitcast_fusion.1.inc_ref = f32[32,88,512]{2,1,0:T(8,128)} fusion(f32[32,112,512]{2,1,0:T(8,128)} %get-tuple-element.48, f32[112,112]{1,0:T(8,128)S(1)} %get-tuple-element.50), kind=kOutput, calls=%fused_computation.1 | convolution fusion | flops 1937768448 | bytes 13152256 | tf_op jit(solution)/shard_map/cond/branch_0_fun/kr,frw->fkw/dot_general | solution.py:604
  71.1 132.6 %circles88.1 = f32[32,88,512]{2,1,0:T(8,128)} custom-call(f32[32,88,512]{2,1,0:T(8,128)} %convolution_bitcast_fusion.1.inc_ref, f32[1,17,88,128]{3,2,1,0:T(8,128)} %convolution_bitcast_fusion.2.damp_ref, f32[2,17,128]{2,1,0:T(8,128)S(1)} %get-tuple-element.53.twid_ref, bf16[2,256,256]{2,1,0:T(8,128)(2,1)S(1)} %get-tuple-element.54.fwd_ref, ...), custom_call_target="tpu_custom_call" | custom-call | tf_op jit(solution)/shard_map/cond/branch_0_fun/circles88/pallas_call | solution.py:525
  203.8 10.0 %convolution_bitcast_fusion = f32[32,112,512]{2,1,0:T(8,128)} fusion(f32[32,88,512]{2,1,0:T(8,128)} %circles88.1, f32[112,112]{1,0:T(8,128)S(1)} %get-tuple-element.50), kind=kOutput, calls=%fused_computation | convolution fusion | flops 1937768448 | bytes 13152256 | tf_op jit(solution)/shard_map/cond/branch_0_fun/kr,fkw->frw/dot_general | solution.py:606
  213.8 13.8 %bitcast_add_fusion = f32[32,112,512]{2,1,0:T(8,128)} fusion(f32[4,8,112,512]{3,2,1,0:T(8,128)} %state_ref.1, f32[32,112,512]{2,1,0:T(8,128)} %get-tuple-element.125, f32[32,112,512]{2,1,0:T(8,128)} %step.1, pred[112]{0:T(512)(128)(4,1)S(1)} %compare_and_fusion), kind=kLoop, calls=%fused_computation.26 | loop fusion | flops 3670016 | bytes 29360240 | tf_op jit(solution)/shard_map/add | solution.py:613
  (11 shorter events, 0.2 us)
Async XLA Ops:
  0.7 58.6 %collective-permute-start = (s32[2,112]{1,0:T(2,128)S(1)}, s32[2,112]{1,0:T(2,128)S(1)}, u32[]{:S(2)}, u32[]{:S(2)}) collective-permute-start(s32[2,112]{1,0:T(2,128)S(1)} %pad_add_fusion), channel_id=1, source_target_pairs={{0,8},{8,0},{16,24},{24,16},{1,9},{9,1},{17,25},{25,17},{2,10},{10... | collective-permute-start | bytes 2696 | tf_op jit(solution)/shard_map/ppermute | solution.py:572
  26.5 32.8 %copy-start.3 = (s32[112]{0:T(128)S(1)}, s32[112]{0:T(128)}, u32[]{:S(2)}) copy-start(s32[112]{0:T(128)} %param.23) | copy-start | bytes 1348
  26.5 32.8 %copy-start.4 = (s32[112]{0:T(128)S(1)}, s32[112]{0:T(128)}, u32[]{:S(2)}) copy-start(s32[112]{0:T(128)} %param.24) | copy-start | bytes 1348
  26.5 33.3 %copy-start = (bf16[2,256,256]{2,1,0:T(8,128)(2,1)S(1)}, bf16[2,256,256]{2,1,0:T(8,128)(2,1)}, u32[]{:S(2)}) copy-start(bf16[2,256,256]{2,1,0:T(8,128)(2,1)} %constant.72.clone) | copy-start | bytes 786436
  26.5 33.3 %copy-start.1 = (bf16[2,256,256]{2,1,0:T(8,128)(2,1)S(1)}, bf16[2,256,256]{2,1,0:T(8,128)(2,1)}, u32[]{:S(2)}) copy-start(bf16[2,256,256]{2,1,0:T(8,128)(2,1)} %constant.71.clone) | copy-start | bytes 786436
  26.5 33.3 %copy-start.2 = (f32[2,17,128]{2,1,0:T(8,128)S(1)}, f32[2,17,128]{2,1,0:T(8,128)}, u32[]{:S(2)}) copy-start(f32[2,17,128]{2,1,0:T(8,128)} %constant.70.clone) | copy-start | bytes 52228

commit v5 on v4

--- a/solution.py
+++ b/solution.py
@@ -543,6 +543,37 @@
     )(inc, weights, twiddle, forward, backward)
 
 
+def finish_kernel(mover_ref, mask_ref, packed_ref, inc_ref, state_ref, out_ref):
+    width = state_ref.shape[2]
+    take = wide(mask_ref[...], width) > 0.5
+    for f in range(state_ref.shape[0]):
+        x = packed_ref[f]
+        high = x.astype(jnp.bfloat16)
+        rest = x - high.astype(jnp.float32)
+        middle = rest.astype(jnp.bfloat16)
+        low = (rest - middle.astype(jnp.float32)).astype(jnp.bfloat16)
+        dot = functools.partial(jnp.dot, mover_ref[...], preferred_element_type=jnp.float32)
+        smooth = (dot(high) + dot(middle)) + dot(low)
+        out_ref[f] = state_ref[f] + jnp.where(take, smooth, inc_ref[f])
+
+
+def finish(mover, mask, packed, inc, state):
+    stacks, rows, width = inc.shape
+    kept = packed.shape[1]
+    group = 4
+    whole = lambda *shape: pl.BlockSpec(shape, lambda i: (0, 0))
+    block = lambda height: pl.BlockSpec((group, height, width), lambda i: (i, 0, 0))
+    return pl.pallas_call(
+        finish_kernel,
+        grid=(stacks // group,),
+        out_shape=jax.ShapeDtypeStruct(inc.shape, jnp.float32),
+        in_specs=[whole(rows, kept), whole(rows, INNER), block(kept), block(rows), block(rows)],
+        out_specs=block(rows),
+        compiler_params=pltpu.CompilerParams(vmem_limit_bytes=40 * 1024 * 1024),
+        name=f"finish{kept}",
+    )(mover, mask, packed, inc, state)
+
+
 def per_device(state, level_courant, damp_table, row_flag, row_table, partner):
     fields_n, levels_n, rows_n, cols_n = state.shape
     na = lax.axis_size("lat")
@@ -594,23 +625,21 @@
 
     def smoothed(ident, kept, inc):
         parts = fewest if kept % 16 else 2
-        mover = None if kept == rows_n else packing[:kept]
-        choice = pick if mover is None else jnp.dot(mover, pick, precision=exact)
+        mover = packing[:kept]
+        choice = jnp.dot(mover, pick, precision=exact)
         weights = jnp.einsum(
             "hrt,tkm->hkrm", choice.reshape(parts, kept // parts, count), grid, precision=exact
         )
-        if mover is None:
-            return filter_circles(inc, weights, parts, ident)
         packed = jnp.einsum("kr,frw->fkw", mover, inc, precision=exact)
         packed = filter_circles(packed, weights, parts, ident)
-        return jnp.einsum("kr,fkw->frw", mover, packed, precision=exact)
-
+        return finish(mover.T.astype(jnp.bfloat16), mask, packed, inc, state.reshape(inc.shape))
+
+    chosen = (active & (row_flag == 1)).astype(jnp.float32)
+    mask = jnp.broadcast_to(chosen[:, None], (rows_n, INNER))
     branch = sum((fullest > size).astype(jnp.int32) for size in sizes[:-1])
-    smooth = lax.switch(
+    result = lax.switch(
         branch, [functools.partial(smoothed, 1 + n, size) for n, size in enumerate(sizes)], inc
     )
-    chosen = (active & (row_flag == 1))[None, :, None]
-    result = state.reshape(inc.shape) + jnp.where(chosen, smooth, inc)
     return result.reshape(state.shape)
 
 

time: 228 us -> 219 us (0.961)
  other arithmetic: 17.1 us -> 3.43 us
  Pallas kernels: 165 us -> 177 us
  matrix products: 24.5 us -> 14.6 us
  local copies, waits for them, and re-layouts: 10.6 us -> 13.3 us
    add x1 -> x0, other arithmetic: 13.8 us -> none  [per_device(): result = state.reshape(inc.shape) + jnp.where(chosen, smooth, inc)]
    pallas_call x0 -> x1, Pallas kernels: none -> 11.5 us  [finish(): pl.pallas_call(finish_kernel, grid=(stacks // group,), out_shape=jax.Shap...]
    dot_general x2 -> x1, matrix products: 10.1 us -> 0.15 us  [smoothed(): choice = jnp.dot(mover, pick, precision=exact)]
    cond x0 -> x2, local copies, waits for them, and re-layouts: none -> 2.64 us
  transfers between devices with their start and end apart: 1 -> 1, of which waited for: 0 -> 0; matrix products, arithmetic and copies ran while one was open for 7% -> 7% of each run, Pallas kernels for 14% -> 15%
where the time goes in v5:
time: 219 us; the launch traced here: 218 us
  Pallas kernels  177 us (81%)
  matrix products  14.6 us (7%)
  local copies, waits for them, and re-layouts  13.3 us (6%)
  blocking collectives  4.93 us (2%)
  between operations  4.91 us (2%)
  other arithmetic  3.43 us (2%)
    pallas_call x1, Pallas kernels, filter_circles(): pl.pallas_call(functools.partial(circle_kernel, upd, parts), out_shape=ja...  133 us
    pallas_call x1, Pallas kernels, increments_of(): pl.pallas_call(step_kernel, out_shape=jax.ShapeDtypeStruct((fields * leve...  32.7 us
    pallas_call x1, Pallas kernels, finish(): pl.pallas_call(finish_kernel, grid=(stacks // group,), out_shape=jax.Shap...  11.5 us
    dot_general x1, matrix products, smoothed(): packed = jnp.einsum('kr,frw->fkw', mover, inc, precision=exact)  9.48 us
    unnamed x1, blocking collectives  4.93 us
  transfers between devices with their start and end apart: 1, of which 0 were waited for; matrix products, arithmetic and copies ran while one was open for 7% of the time, Pallas kernels for 15%

profile of v5, /device:TPU:10, one launch (start us, length us, event | category | flops | bytes accessed | tf_op | source)
XLA Modules:
  0.0 218.3 jit_solution(2778137234612455892)
XLA Ops:
  0.0 0.7 pad_add_fusion
  0.7 0.0 collective-permute-start
  1.2 0.6 fusion.31
  1.8 0.6 fusion.30
  2.4 0.7 convert_element_type.77
  3.1 0.7 and_convert_fusion
  3.7 1.1 reshape.107
  4.8 1.0 concatenate.6
  5.8 0.2 reshape.106
  6.0 0.2 copy.84
  6.2 1.2 dynamic-slice
  8.1 0.9 dynamic-update-slice
  9.0 4.9 %all-reduce.2 = s32[448]{0:T(512)S(1)} all-reduce(s32[448]{0:T(512)S(1)} %dynamic-update-slice), channel_id=2, replica_groups=mesh['lat'=4,'lon'=8] {'lat'}, use_global_device_ids=true, to_apply=%add.2 | all-reduce | flops 448 | bytes 3584
  13.9 0.1 reshape.120
  14.0 0.1 reduce_sum.9
  14.1 0.6 reduce_max.9
  18.5 2.1 fusion.20
  20.7 1.1 convolution_bitcast_fusion.7
  21.7 0.1 pad_maximum_fusion
  21.9 0.7 pad.5
  22.5 0.7 stack.42.ends_ref
  23.2 0.8 broadcast_in_dim.10.geo_ref
  24.0 0.6 broadcast_in_dim.13.meet_ref
  24.6 0.6 broadcast_in_dim.12.clane_ref
  25.2 1.3 broadcast_in_dim.11.ccol_ref
  26.5 0.0 copy-start.3
  26.5 0.0 copy-start.4
  26.5 32.7 %step.1 = f32[32,112,512]{2,1,0:T(8,128)} custom-call(f32[8]{0:T(128)} %c_ref.1, f32[6]{0:T(128)} %stack.42.ends_ref, f32[4,8,112,512]{3,2,1,0:T(8,128)} %state_ref.1, f32[3,112,128]{2,1,0:T(8,128)} %broadcast_in_dim.10.geo_ref, f32[8,128]{1,0:T(8,128)} %broadcast_in_dim.11.ccol_ref, f32[8,128]{1,0:T(8,128)} %broadcast_in_dim.12.clane_ref, ...), custom_call_target="tpu_custom_call" | custom-call | tf_op jit(solution)/shard_map/step/pallas_call | solution.py:248
  59.2 0.0 collective-permute-done
  59.2 0.0 copy-done.3
  59.2 0.0 copy-done.4
  59.3 0.1 copy.66
  59.4 0.2 reduce-window.8
  59.5 0.1 add_reduce_fusion
  59.7 0.1 fusion.23
  59.8 158.5 %conditional.1 = (f32[4,8,112,512]{3,2,1,0:T(8,128)}) conditional(s32[]{:T(128)} %clamp.3, (f32[112,112]{0,1:T(8,128)S(1)}, f32[32,112,512]{2,1,0:T(8,128)}, f32[112,16]{0,1:T(8,128)S(1)}, f32[16,17,128]{2,1,0:T(8,128)S(1)}, f32[4,8,112,512]{3,2,1,0:T(8,128)}, /*index=5*/f32[112]{0:T(128)S(1)}) %tuple.46, ...), branch_computations={%region_3.4_spmd.clone, %region_4.5_spmd.clone, %region_5.6_spmd.c... | conditional | flops 2515499264 | bytes 45423588 | solution.py:640
  59.8 9.5 %convolution_bitcast_fusion.inc_ref = f32[32,88,512]{2,1,0:T(8,128)} fusion(f32[32,112,512]{2,1,0:T(8,128)} %get-tuple-element.123.inc_ref, f32[112,112]{0,1:T(8,128)S(1)} %get-tuple-element.122), kind=kOutput, calls=%fused_computation | convolution fusion | flops 1937768448 | bytes 13157376 | tf_op jit(solution)/shard_map/cond/branch_0_fun/kr,frw->fkw/dot_general | solution.py:633
  69.3 0.2 convolution_bitcast_fusion.2
  69.4 1.8 convolution_bitcast_fusion.1.damp_ref
  71.2 132.8 %circles88.1.packed_ref = f32[32,88,512]{2,1,0:T(8,128)} custom-call(f32[32,88,512]{2,1,0:T(8,128)} %convolution_bitcast_fusion.inc_ref, f32[1,17,88,128]{3,2,1,0:T(8,128)} %convolution_bitcast_fusion.1.damp_ref, f32[2,17,128]{2,1,0:T(8,128)} %constant.70.clone.4.twid_ref, bf16[2,256,256]{2,1,0:T(8,128)(2,1)} %constant.71.clone.4.fwd_ref, ...), custom_call_target="tpu_custom_call" | custom-call | tf_op jit(solution)/shard_map/cond/branch_0_fun/circles88/pallas_call | solution.py:525
  204.0 0.1 broadcast_in_dim.18.mask_ref
  204.1 0.0 copy-start.2
  204.1 2.6 %copy-done.2 = f32[32,88,512]{2,1,0:T(8,128)S(1)} copy-done((f32[32,88,512]{2,1,0:T(8,128)S(1)}, f32[32,88,512]{2,1,0:T(8,128)}, u32[]{:S(2)}) %copy-start.2) | copy-done | bytes 5767192 | tf_op jit(solution)/shard_map/cond
  206.7 11.5 %finish88.1 = f32[32,112,512]{2,1,0:T(8,128)} custom-call(bf16[112,88]{1,0:T(8,128)(2,1)S(1)} %fusion.4.mover_ref, f32[112,128]{1,0:T(8,128)S(1)} %broadcast_in_dim.18.mask_ref, f32[32,88,512]{2,1,0:T(8,128)S(1)} %copy-done.2, f32[32,112,512]{2,1,0:T(8,128)} %get-tuple-element.123.inc_ref, f32[32,112,512]{2,1,0:T(8,128)} %bitcast.86), custom_call_target="tpu_custom_call" | custom-call | tf_op jit(solution)/shard_map/cond/branch_0_fun/finish88/pallas_call | solution.py:566
  (11 shorter events, 0.2 us)
Async XLA Ops:
  0.7 58.5 %collective-permute-start = (s32[2,112]{1,0:T(2,128)S(1)}, s32[2,112]{1,0:T(2,128)S(1)}, u32[]{:S(2)}, u32[]{:S(2)}) collective-permute-start(s32[2,112]{1,0:T(2,128)S(1)} %pad_add_fusion), channel_id=1, source_target_pairs={{0,8},{8,0},{16,24},{24,16},{1,9},{9,1},{17,25},{25,17},{2,10},{10... | collective-permute-start | bytes 2696 | tf_op jit(solution)/shard_map/ppermute | solution.py:603
  26.5 32.7 %copy-start.3 = (s32[112]{0:T(128)S(1)}, s32[112]{0:T(128)}, u32[]{:S(2)}) copy-start(s32[112]{0:T(128)} %param.23) | copy-start | bytes 1348
  26.5 32.7 %copy-start.4 = (s32[112]{0:T(128)S(1)}, s32[112]{0:T(128)}, u32[]{:S(2)}) copy-start(s32[112]{0:T(128)} %param.24) | copy-start | bytes 1348
  204.1 2.6 %copy-start.2 = (f32[32,88,512]{2,1,0:T(8,128)S(1)}, f32[32,88,512]{2,1,0:T(8,128)}, u32[]{:S(2)}) copy-start(f32[32,88,512]{2,1,0:T(8,128)} %circles88.1.packed_ref) | copy-start | bytes 17301508 | tf_op jit(solution)/shard_map/cond
